TPU v7x, 256 devices: a whole 4x4x8 slice. The times are simulated.
256 devices in a mesh: mode: 4 (over x), rest: 64 (over y, z, core).
Axes of the slice: x: 4, y: 4, z: 8, core: 2. Of those that a mesh axis runs over, the one named last changes fastest.
Arguments:
- unfolded: float32 [512, 524288], P('mode', 'rest'), may hold values from -150 to 150
- start_block: float32 [512, 128], replicated, may hold values from -6 to 6
Outputs:
- triangle: float32 [512, 512], replicated
- factor: float32 [512, 128], replicated
- core: float32 [128, 524288], P('mode', 'rest')
All inputs are finite; a program needn't handle non-finite values.
Results may differ from a plain program's by a relative error of at most 0.0003.
Values sent between devices are 32-bit elements; how exact they have to be, the bound alone decides.
No kernel may reach another device: no remote copies, remote signals or barrier semaphores. Data moves between devices by JAX's collectives and lax.ppermute only.
A program may use at most 64 MiB of HBM per device.

v0:
```python
import jax
import jax.numpy as jnp
from jax import lax
from jax.sharding import PartitionSpec as P

ITERS = 3


def orthogonal_steps(triangle, start_block, repeats):
    highest = lax.Precision.HIGHEST
    columns_now = start_block
    for repeat in range(repeats):
        inner = jnp.dot(triangle.T, columns_now, precision=highest)
        image = jnp.dot(triangle, inner, precision=highest)
        projected = jnp.dot(image.T, image, precision=highest)
        small_factor = jnp.linalg.cholesky(projected)
        columns_now = lax.linalg.triangular_solve(
            small_factor, image, left_side=False, lower=True, transpose_a=True
        )
    return columns_now


def per_device(unfolded, start_block):
    highest = lax.Precision.HIGHEST
    rows_dev, cols_dev = unfolded.shape
    total_cols = cols_dev * lax.axis_size("rest")
    full_rows = lax.all_to_all(unfolded, "mode", split_axis=1, concat_axis=0, tiled=True)
    gram_part = jnp.dot(full_rows, full_rows.T, precision=highest) / total_cols
    gram = lax.psum(gram_part, ("mode", "rest"))
    triangle = jnp.linalg.cholesky(gram)
    factor = orthogonal_steps(triangle, start_block, ITERS)
    partial_value = jnp.dot(factor.T, full_rows, precision=highest)
    core = lax.all_to_all(partial_value, "mode", split_axis=0, concat_axis=1, tiled=True)
    return (triangle, factor, core)


def solution(mesh):
    return jax.shard_map(
        per_device,
        mesh=mesh,
        in_specs=(P("mode", "rest"), P()),
        out_specs=(P(), P(), P("mode", "rest")),
        check_vma=False,
    )
```

profile of v0, /device:TPU:6, one launch (start us, length us, event | category | flops | bytes accessed | tf_op | source)
XLA Modules:
  0.0 527.4 jit_solution(3555311990880964987)
XLA Ops:
  7.2 2.5 copy.24
  9.7 51.3 %all_to_all.35 = f32[128,4,2048]{2,0,1:T(8,128)S(1)} all-to-all(f32[128,4,2048]{2,0,1:T(8,128)S(1)} %bitcast.96), channel_id=1, replica_groups=mesh['mode'=4,'rest'=64] {'mode'}, dimensions={1} | all-to-all | bytes 8388608 | tf_op jit(solution)/shard_map/all_to_all | solution.py:27
  61.0 1.9 copy-done.1
  63.0 7.9 %convolution_multiply_fusion = f32[512,512]{0,1:T(8,128)} fusion(f32[512,2048]{1,0:T(8,128)S(1)} %bitcast.94), kind=kOutput, calls=%fused_computation.1 | convolution fusion | flops 6442713088 | bytes 5242880 | tf_op jit(solution)/shard_map/dot_general | solution.py:28
  70.9 258.8 %all-reduce.3.cloned.1.call-done = f32[512,512]{0,1:T(8,128)} async-done(((f32[512,512]{0,1:T(8,128)}), f32[512,512]{0,1:T(8,128)}) %all-reduce.3.cloned.1.call-update) | async-done | bytes 1048592 | tf_op jit(solution)/shard_map/psum | solution.py:29
  329.7 1.6 copy.14
  331.3 1.4 fusion
  332.7 11.7 %cholesky.120 = f32[128,128]{1,0:T(8,128)S(1)} custom-call(f32[128,128]{1,0:T(8,128)S(1)} %cholesky.356), custom_call_target="Cholesky" | custom-call | tf_op jit(solution)/shard_map/jit(cholesky)/cholesky | solution.py:30
  344.5 10.2 %custom-call.32 = f32[1,128,128]{1,2,0:T(8,128)S(1)} custom-call(f32[1,128,128]{2,1,0:T(8,128)S(1)} %get-tuple-element.20), custom_call_target="InvertDiagBlocksLowerTriangular" | custom-call | tf_op jit(solution)/shard_map/jit(cholesky)/cholesky | solution.py:30
  355.5 11.7 %cholesky.244 = f32[128,128]{1,0:T(8,128)S(1)} custom-call(f32[128,128]{1,0:T(8,128)S(1)} %cholesky.360), custom_call_target="Cholesky" | custom-call | tf_op jit(solution)/shard_map/jit(cholesky)/cholesky | solution.py:30
  367.2 9.8 %custom-call.33 = f32[1,128,128]{1,2,0:T(8,128)S(1)} custom-call(f32[1,128,128]{2,1,0:T(8,128)S(1)} %get-tuple-element.17), custom_call_target="InvertDiagBlocksLowerTriangular" | custom-call | tf_op jit(solution)/shard_map/jit(cholesky)/cholesky | solution.py:30
  377.3 0.4 convolution_subtract_fusion.1
  377.7 11.9 %cholesky.265 = f32[128,128]{1,0:T(8,128)S(1)} custom-call(f32[128,128]{1,0:T(8,128)S(1)} %cholesky.365), custom_call_target="Cholesky" | custom-call | tf_op jit(solution)/shard_map/jit(cholesky)/cholesky | solution.py:30
  389.6 0.6 compare_reduce_fusion.4
  390.3 9.8 %custom-call.34 = f32[1,128,128]{1,2,0:T(8,128)S(1)} custom-call(f32[1,128,128]{2,1,0:T(8,128)S(1)} %get-tuple-element.14), custom_call_target="InvertDiagBlocksLowerTriangular" | custom-call | tf_op jit(solution)/shard_map/jit(cholesky)/cholesky | solution.py:30
  400.3 0.4 convolution_subtract_fusion.2
  400.7 11.7 %cholesky.282 = f32[128,128]{1,0:T(8,128)S(1)} custom-call(f32[128,128]{1,0:T(8,128)S(1)} %convolution_subtract_fusion.2), custom_call_target="Cholesky" | custom-call | tf_op jit(solution)/shard_map/jit(cholesky)/cholesky | solution.py:30
  412.4 0.7 compare_reduce_fusion.3
  413.1 0.6 compare_reduce_fusion.5
  416.4 1.8 fusion.22
  418.2 1.0 fusion.23
  419.2 0.6 fusion.24
  419.9 11.9 %cholesky.325 = f32[128,128]{1,0:T(8,128)S(1)} custom-call(f32[128,128]{1,0:T(8,128)S(1)} %fusion.18), custom_call_target="Cholesky" | custom-call | tf_op jit(solution)/shard_map/jit(cholesky)/cholesky | solution.py:16
  431.9 0.6 compare_reduce_fusion.2
  432.5 0.7 fusion.7
  433.2 9.8 %custom-call.37 = f32[1,128,128]{1,2,0:T(8,128)S(1)} custom-call(f32[1,128,128]{2,1,0:T(8,128)S(1)} %fusion.7), custom_call_target="InvertDiagBlocksLowerTriangular" | custom-call | tf_op jit(solution)/shard_map/triangular_solve/custom-call.8 | solution.py:17
  443.0 0.4 convolution_bitcast_fusion.1
  443.4 1.8 fusion.25
  445.2 1.0 fusion.26
  446.2 0.6 fusion.27
  446.9 11.7 %cholesky.336 = f32[128,128]{1,0:T(8,128)S(1)} custom-call(f32[128,128]{1,0:T(8,128)S(1)} %fusion.16), custom_call_target="Cholesky" | custom-call | tf_op jit(solution)/shard_map/jit(cholesky)/cholesky | solution.py:16
  458.7 0.6 compare_reduce_fusion.1
  459.3 0.7 fusion.8
  460.0 10.2 %custom-call.38 = f32[1,128,128]{1,2,0:T(8,128)S(1)} custom-call(f32[1,128,128]{2,1,0:T(8,128)S(1)} %fusion.8), custom_call_target="InvertDiagBlocksLowerTriangular" | custom-call | tf_op jit(solution)/shard_map/triangular_solve/custom-call.8 | solution.py:17
  470.2 0.4 convolution_bitcast_fusion
  470.6 1.8 fusion.28
  472.4 1.0 fusion.29
  473.4 0.6 fusion.30
  474.1 11.7 %cholesky.347 = f32[128,128]{1,0:T(8,128)S(1)} custom-call(f32[128,128]{1,0:T(8,128)S(1)} %fusion.14), custom_call_target="Cholesky" | custom-call | tf_op jit(solution)/shard_map/jit(cholesky)/cholesky | solution.py:16
  485.9 0.6 compare_reduce_fusion
  486.5 0.7 fusion.9
  487.2 9.8 %custom-call.39 = f32[1,128,128]{1,2,0:T(8,128)S(1)} custom-call(f32[1,128,128]{2,1,0:T(8,128)S(1)} %fusion.9), custom_call_target="InvertDiagBlocksLowerTriangular" | custom-call | tf_op jit(solution)/shard_map/triangular_solve/custom-call.8 | solution.py:17
  497.0 0.6 fusion.12
  497.6 5.5 %fusion.31 = f32[4,32,2048]{2,1,0:T(8,128)} fusion(f32[4,32,512]{2,1,0:T(8,128)S(1)} %bitcast.99, f32[512,2048,1]{1,0,2:T(8,128)} %bitcast.95), kind=kOutput, calls=%fused_computation.72 | convolution fusion | flops 1610612736 | bytes 5505024 | tf_op jit(solution)/shard_map/dot_general | solution.py:32
  503.1 4.8 all-to-all-start.1
  507.9 0.8 copy.19
  508.7 10.6 %all-to-all-done.1 = f32[4,32,2048]{2,1,0:T(8,128)S(1)} async-done(((f32[4,32,2048]{2,1,0:T(8,128)}), f32[4,32,2048]{2,1,0:T(8,128)S(1)}, u32[]{:S(2)}, u32[]{:S(2)}) %all-to-all-start.1) | async-done | bytes 1048608 | tf_op jit(solution)/shard_map/all_to_all | solution.py:33
  519.3 1.0 copy.22
  (29 shorter events, 2.0 us)
Async XLA Ops:
  7.2 409.2 %copy-start = (f32[512,128]{1,0:T(8,128)S(1)}, f32[512,128]{1,0:T(8,128)}, u32[]{:S(2)}) copy-start(f32[512,128]{1,0:T(8,128)} %param.6) | copy-start | bytes 786436
  7.2 322.5 %all-reduce.3.cloned.1.call-start = ((), (), s32[]{:S(2)}) async-start(), calls=%async_computation.2 | async-start | bytes 2097152 | tf_op jit(solution)/shard_map/psum | solution.py:29
  61.0 1.9 copy-start.1
  416.4 56.0 %copy-start.2 = (f32[512,512]{1,0:T(8,128)}, f32[512,512]{1,0:T(8,128)S(1)}, u32[]{:S(2)}) copy-start(f32[512,512]{1,0:T(8,128)S(1)} %select_select_fusion) | copy-start | bytes 3145732
  503.1 16.2 %all-to-all-start.1 = ((f32[4,32,2048]{2,1,0:T(8,128)}), f32[4,32,2048]{2,1,0:T(8,128)S(1)}, u32[]{:S(2)}, u32[]{:S(2)}) async-start(f32[4,32,2048]{2,1,0:T(8,128)} %fusion.31), calls=%async_computation.1 | async-start | bytes 2097152 | tf_op jit(solution)/shard_map/all_to_all | solution.py:33
Sparse Core Ops, SparseCore 0:
  71.0 258.6 all-reduce.2
where the time goes:
time: 538 us; the launch traced here: 527 us
  waiting for transfers between devices  269 us (50%)
  other arithmetic  150 us (28%)
  blocking collectives  51.3 us (10%)
  matrix products  26.8 us (5%)
  between operations  17.1 us (3%)
  local copies, waits for them, and re-layouts  8.27 us (2%)
    psum x1, waiting for transfers between devices, per_device(): gram = lax.psum(gram_part, ('mode', 'rest'))  259 us
    another operation x14, other arithmetic, per_device(): triangle = jnp.linalg.cholesky(gram)  78.9 us
    all_to_all x1, blocking collectives, per_device(): lax.all_to_all(unfolded, 'mode', split_axis=1, concat_axis=0, tiled=True)  51.3 us
    another operation x9, other arithmetic, orthogonal_steps(): small_factor = jnp.linalg.cholesky(projected)  37.4 us
    another operation x6, other arithmetic, orthogonal_steps(): lax.linalg.triangular_solve(small_factor, image, left_side=False, lower=T...  31.8 us
  transfers between devices with their start and end apart: 2, of which 2 were waited for; matrix products, arithmetic and copies ran while one was open for 0% of the time, Pallas kernels for 0%

commit v1 on v0

v1 whole, which is shorter than its diff:
```python
import functools

import jax
import jax.numpy as jnp
from jax import lax
from jax.experimental import pallas as pl
from jax.experimental.pallas import tpu as pltpu
from jax.sharding import Mesh, PartitionSpec as P

ITERS = 3
HIGHEST = lax.Precision.HIGHEST
NB = 128
NT = (((1,), (1,)), ((), ()))
TN = (((0,), (0,)), ((), ()))
F32 = jnp.float32


def dot_exact(a, b, dims=(((1,), (0,)), ((), ()))):
    return lax.dot_general(a, b, dims, precision=HIGHEST, preferred_element_type=F32)


def cholesky_block(matrix, inverse_ref, upper_ref=None):
    n = matrix.shape[0]
    shape = (8, n)
    spread = functools.partial(jnp.broadcast_to, shape=shape)
    lane = lax.broadcasted_iota(jnp.int32, shape, 1)
    sub = lax.broadcasted_iota(jnp.int32, shape, 0)
    rows = [matrix[8 * i : 8 * i + 8, :] for i in range(n // 8)]
    for t in range(n // 8):
        first = 8 * t
        inside = (lane >= first) & (lane < first + 8)
        cols = {
            i: [spread(rows[i][:, first + j : first + j + 1]) for j in range(8)]
            for i in range(t, n // 8)
        }
        own = cols[t]
        top = rows[t]
        unit = jnp.where(lane == first + sub, 1.0, 0.0)
        recips = []
        mults = {i: [] for i in range(t + 1, n // 8)}
        for j in range(8):
            recip = 1.0 / spread(own[j][j : j + 1, :])
            recips.append(recip)
            mult = jnp.where(sub > j, own[j] * recip, 0.0)
            top = top - mult * spread(top[j : j + 1, :])
            unit = unit - mult * spread(unit[j : j + 1, :])
            pivot_row = {l: spread(own[l][j : j + 1, :]) for l in range(j + 1, 8)}
            for i in range(t + 1, n // 8):
                mult = cols[i][j] * recip
                mults[i].append(mult)
                for l in range(j + 1, 8):
                    cols[i][l] = cols[i][l] - mult * pivot_row[l]
            for l in range(j + 1, 8):
                own[l] = own[l] - (own[j] * pivot_row[l]) * recip
        scale = recips[0]
        for j in range(1, 8):
            scale = jnp.where(sub == j, recips[j], scale)
        scale = lax.rsqrt(1.0 / scale)
        inverse_ref[first : first + 8, :] = scale * jnp.where(lane < first, top, unit)
        if upper_ref is not None:
            upper_ref[first : first + 8, :] = jnp.where(lane >= first + sub, scale * top, 0.0)
        source = jnp.where(inside, unit, top)
        for i in range(t + 1, n // 8):
            left = jnp.where(inside, 0.0, rows[i])
            for j in range(8):
                left = left - mults[i][j] * spread(source[j : j + 1, :])
            rows[i] = left


def block_index(i, j):
    return i * (i + 1) // 2 + j


def gram_kernel(x_ref, out_ref, acc_ref):
    step = pl.program_id(0)
    m = x_ref.shape[0]
    half = m // 2
    x = x_ref[...]
    high = x.astype(jnp.bfloat16)
    low = (x - high.astype(F32)).astype(jnp.bfloat16)

    def product(r, c):
        dot = functools.partial(lax.dot_general, dimension_numbers=NT, preferred_element_type=F32)
        small = dot(low[r], low[c]) + (dot(high[r], low[c]) + dot(low[r], high[c]))
        return dot(high[r], high[c]) + small

    upper, lower, whole = slice(0, half), slice(half, m), slice(0, m)

    @pl.when(step == 0)
    def _():
        acc_ref[upper, upper] = product(upper, upper)
        acc_ref[lower, whole] = product(lower, whole)

    @pl.when(step > 0)
    def _():
        acc_ref[upper, upper] += product(upper, upper)
        acc_ref[lower, whole] += product(lower, whole)

    @pl.when(step == pl.num_programs(0) - 1)
    def _():
        for i in range(m // NB):
            for j in range(i + 1):
                b = block_index(i, j)
                out_ref[b * NB : (b + 1) * NB, :] = acc_ref[i * NB : (i + 1) * NB, j * NB : (j + 1) * NB]


def gram_lower(full_rows):
    m, cols = full_rows.shape
    nblk = m // NB
    rows_out = nblk * (nblk + 1) // 2 * NB
    tile = min(512, cols)
    return pl.pallas_call(
        gram_kernel,
        grid=(cols // tile,),
        in_specs=[pl.BlockSpec((m, tile), lambda k: (0, k))],
        out_specs=pl.BlockSpec((rows_out, NB), lambda k: (0, 0)),
        out_shape=jax.ShapeDtypeStruct((rows_out, NB), F32),
        scratch_shapes=[pltpu.VMEM((m, m), F32)],
        compiler_params=pltpu.CompilerParams(vmem_limit_bytes=48 << 20),
        name="gram_lower",
    )(full_rows)


def factor_kernel(scale, core_ref, gram_ref, start_ref, tri_ref, basis_ref, full_ref, inv_ref, up_ref):
    m = tri_ref.shape[0]
    nblk = m // NB

    def sl(i):
        return slice(i * NB, (i + 1) * NB)

    def block(i, j):
        return gram_ref[sl(block_index(i, j)), :] * scale

    @pl.when(core_ref[0] == 0)
    def _():
        for i in range(nblk):
            for j in range(i + 1):
                full_ref[sl(i), sl(j)] = block(i, j)
        for p in range(nblk):
            cholesky_block(full_ref[sl(p), sl(p)], inv_ref, up_ref)
            tri_ref[sl(p), sl(p)] = up_ref[...].T
            for i in range(p):
                tri_ref[sl(i), sl(p)] = jnp.zeros((NB, NB), F32)
            if p + 1 < nblk:
                below = dot_exact(full_ref[(p + 1) * NB :, sl(p)], inv_ref[...], NT)
                tri_ref[(p + 1) * NB :, sl(p)] = below
                for j in range(p + 1, nblk):
                    lo = (j - p - 1) * NB
                    full_ref[j * NB :, sl(j)] -= dot_exact(below[lo:, :], below[lo : lo + NB, :], NT)

    @pl.when(core_ref[0] != 0)
    def _():
        for i in range(nblk):
            for j in range(i + 1):
                b = block(i, j)
                full_ref[sl(i), sl(j)] = b
                if j < i:
                    full_ref[sl(j), sl(i)] = b.T
        basis_ref[...] = start_ref[...]

        def step(_, carry):
            image = dot_exact(full_ref[...], basis_ref[...])
            cholesky_block(dot_exact(image, image, TN), inv_ref)
            basis_ref[...] = dot_exact(image, inv_ref[...], NT)
            return carry

        lax.fori_loop(0, ITERS, step, 0)


def factorize(core, gram, start_block, scale):
    m, r = start_block.shape
    vmem = pl.BlockSpec(memory_space=pltpu.VMEM)
    return pl.pallas_call(
        functools.partial(factor_kernel, scale),
        in_specs=[pl.BlockSpec(memory_space=pltpu.SMEM), vmem, vmem],
        out_specs=[vmem, vmem],
        out_shape=[jax.ShapeDtypeStruct((m, m), F32), jax.ShapeDtypeStruct((m, r), F32)],
        scratch_shapes=[pltpu.VMEM((m, m), F32), pltpu.VMEM((NB, NB), F32), pltpu.VMEM((NB, NB), F32)],
        compiler_params=pltpu.CompilerParams(vmem_limit_bytes=48 << 20),
        name="factorize",
    )(core.reshape(1).astype(jnp.int32), gram, start_block)


def swap_cores(value):
    return lax.ppermute(value, "core", [(0, 1), (1, 0)])


def spread_out(value, axes):
    n = lax.axis_size(axes)
    copies = jnp.broadcast_to(value[None], (n,) + value.shape)
    return lax.all_to_all(copies, axes, 0, 0, tiled=True)


def sum_everywhere(part):
    core = lax.axis_index("core")
    rows, lanes = part.shape
    halves = part.reshape(2, rows // 2, lanes)
    mine = lax.dynamic_index_in_dim(halves, core, 0, keepdims=False)
    other = lax.dynamic_index_in_dim(halves, 1 - core, 0, keepdims=False)
    mine = mine + swap_cores(other)
    plane = ("mode", "y")
    n = lax.axis_size(plane)
    pieces = lax.all_to_all(mine.reshape(n, rows // 2 // n, lanes), plane, 0, 0, tiled=True)
    piece = spread_out(pieces.sum(0), "z").sum(0)
    mine = spread_out(piece, plane).reshape(rows // 2, lanes)
    other = swap_cores(mine)
    first = core == 0
    return jnp.concatenate([jnp.where(first, mine, other), jnp.where(first, other, mine)], axis=0)


def per_device(unfolded, start_block):
    total_cols = unfolded.shape[1] * lax.axis_size(("y", "z", "core"))
    full_rows = lax.all_to_all(unfolded, "mode", split_axis=1, concat_axis=0, tiled=True)
    gram = sum_everywhere(gram_lower(full_rows))
    core_id = lax.axis_index("core")
    tri, basis = factorize(core_id, gram, start_block, 1.0 / total_cols)
    factor = jnp.where(core_id == 1, basis, swap_cores(basis))
    triangle = jnp.where(core_id == 0, tri, swap_cores(tri))
    partial_value = jnp.dot(factor.T, full_rows, precision=HIGHEST)
    core = lax.all_to_all(partial_value, "mode", split_axis=0, concat_axis=1, tiled=True)
    return (triangle, factor, core)


def solution(mesh):
    fine = Mesh(mesh.devices.reshape(4, 4, 8, 2), ("mode", "y", "z", "core"))
    rest = ("y", "z", "core")
    return jax.shard_map(
        per_device,
        mesh=fine,
        in_specs=(P("mode", rest), P()),
        out_specs=(P(), P(), P("mode", rest)),
        check_vma=False,
    )
```

time: 538 us -> 161 us (0.30); the launches traced: 527 us -> 159 us
  waiting for transfers between devices: 269 us -> 49.5 us
  other arithmetic: 150 us -> 1.37 us
  Pallas kernels: 0 us -> 24.5 us
  matrix products: 26.8 us -> 4.55 us
  between operations: 17.1 us -> 0.75 us
  blocking collectives: 51.3 us -> 63 us
    psum x1 -> x0, waiting for transfers between devices: 259 us -> none  [per_device(): gram = lax.psum(gram_part, ('mode', 'rest'))]
    another operation x29 -> x0, other arithmetic: 148 us -> none  [the longest x14 78.9 us: per_device(): triangle = jnp.linalg.cholesky(gram)]
    all_to_all x1, waiting for transfers between devices: 10.6 us -> 45.2 us  [per_device(): lax.all_to_all(unfolded, 'mode', split_axis=1, concat_axis=0, tiled=True)]
    pallas_call x0 -> x2, Pallas kernels: none -> 24.5 us  [the longest x1 18.3 us: factorize(): pl.pallas_call(functools.partial(factor_kernel, scale), in_specs=[pl.Bloc...]
    dot_general x11 -> x1, matrix products: 23.5 us -> 4.55 us  [per_device(): partial_value = jnp.dot(factor.T, full_rows, precision=HIGHEST)]
    all_to_all x1 -> x4, blocking collectives: 51.3 us -> 63 us  [the longest x2 30 us: spread_out(): return lax.all_to_all(copies, axes, 0, 0, tiled=True)]
  transfers between devices with their start and end apart: 2 -> 5, of which waited for: 2 -> 4; matrix products, arithmetic and copies ran while one was open for 0% -> 4% of each run, Pallas kernels for 0% -> 0%
where the time goes in v1:
time: 161 us; the launch traced here: 159 us
  blocking collectives  63 us (39%)
  waiting for transfers between devices  49.5 us (31%)
  Pallas kernels  24.5 us (15%)
  starting transfers between devices  8.93 us (6%)
  local copies, waits for them, and re-layouts  5.93 us (4%)
  matrix products  4.55 us (3%)
    all_to_all x1, waiting for transfers between devices, per_device(): lax.all_to_all(unfolded, 'mode', split_axis=1, concat_axis=0, tiled=True)  45.2 us
    all_to_all x2, blocking collectives, spread_out(): return lax.all_to_all(copies, axes, 0, 0, tiled=True)  30 us
    all_to_all x1, blocking collectives, per_device(): lax.all_to_all(partial_value, 'mode', split_axis=0, concat_axis=1, tiled=...  18.4 us
    pallas_call x1, Pallas kernels, factorize(): pl.pallas_call(functools.partial(factor_kernel, scale), in_specs=[pl.Bloc...  18.3 us
    all_to_all x1, blocking collectives, sum_everywhere(): lax.all_to_all(mine.reshape(n, rows // 2 // n, lanes), plane, 0, 0, tiled...  14.6 us
    all_to_all x1, starting transfers between devices, per_device(): lax.all_to_all(unfolded, 'mode', split_axis=1, concat_axis=0, tiled=True)  7.01 us
    pallas_call x1, Pallas kernels, gram_lower(): pl.pallas_call(gram_kernel, grid=(cols // tile,), in_specs=[pl.BlockSpec(...  6.25 us
    all_to_all x1, local copies, waits for them, and re-layouts, per_device(): lax.all_to_all(unfolded, 'mode', split_axis=1, concat_axis=0, tiled=True)  4.65 us
  transfers between devices with their start and end apart: 5, of which 4 were waited for; matrix products, arithmetic and copies ran while one was open for 4% of the time, Pallas kernels for 0%

profile of v1, /device:TPU:6, one launch (start us, length us, event | category | flops | bytes accessed | tf_op | source)
XLA Modules:
  0.0 158.5 jit_solution(15201056637614276896)
XLA Ops:
  0.6 4.7 %copy.16 = f32[16,4,8,2048]{3,2,0,1:T(8,128)} copy(f32[16,4,8,2048]{3,2,1,0:T(8,128)} %bitcast.29) | data formatting | bytes 8388608 | tf_op jit(solution)/shard_map/all_to_all | solution.py:213
  5.3 7.0 %all-to-all-start = ((f32[128,4,2048]{2,0,1:T(8,128)}), f32[128,4,2048]{2,0,1:T(8,128)}, u32[]{:S(2)}, u32[]{:S(2)}) async-start(f32[128,4,2048]{2,0,1:T(8,128)} %bitcast.28), calls=%async_computation | async-start | bytes 8388608 | tf_op jit(solution)/shard_map/all_to_all | solution.py:213
  12.3 45.2 %all-to-all-done = f32[128,4,2048]{2,0,1:T(8,128)} async-done(((f32[128,4,2048]{2,0,1:T(8,128)}), f32[128,4,2048]{2,0,1:T(8,128)}, u32[]{:S(2)}, u32[]{:S(2)}) %all-to-all-start) | async-done | bytes 4194336 | tf_op jit(solution)/shard_map/all_to_all | solution.py:213
  57.5 6.3 %gram_lower.1 = f32[1280,128]{1,0:T(8,128)S(1)} custom-call(f32[512,2048]{1,0:T(8,128)} %bitcast.2.x_ref), custom_call_target="tpu_custom_call" | custom-call | tf_op jit(solution)/shard_map/gram_lower/pallas_call | solution.py:112
  63.7 0.0 copy-start
  63.8 0.1 collective-permute-start
  63.9 1.6 %collective-permute-done = f32[640,128]{1,0:T(8,128)S(1)} collective-permute-done((f32[640,128]{1,0:T(8,128)S(1)}, f32[640,128]{1,0:T(8,128)S(1)}, u32[]{:S(2)}, u32[]{:S(2)}) %collective-permute-start) | collective-permute-done | bytes 327712 | tf_op jit(solution)/shard_map/ppermute | solution.py:185
  65.5 14.6 %all_to_all.50 = f32[16,40,128]{2,1,0:T(8,128)S(1)} all-to-all(f32[16,40,128]{2,1,0:T(8,128)S(1)} %bitcast.31), channel_id=1, replica_groups=mesh['mode'=4,'y'=4,'z'=8,'core'=2] {'mode','y'}, dimensions={0} | all-to-all | bytes 655360 | tf_op jit(solution)/shard_map/all_to_all | solution.py:203
  80.2 17.7 %all_to_all.51 = f32[8,40,128]{2,1,0:T(8,128)S(1)} all-to-all(f32[8,40,128]{2,1,0:T(8,128)S(1)} %broadcast_in_dim.4), channel_id=1, replica_groups=mesh['mode'=4,'y'=4,'z'=8,'core'=2] {'z'}, dimensions={0} | all-to-all | bytes 327680 | tf_op jit(solution)/shard_map/all_to_all | solution.py:191
  97.9 12.3 %all_to_all.52 = f32[16,40,128]{2,1,0:T(8,128)S(1)} all-to-all(f32[16,40,128]{2,1,0:T(8,128)S(1)} %broadcast_in_dim.5), channel_id=1, replica_groups=mesh['mode'=4,'y'=4,'z'=8,'core'=2] {'mode','y'}, dimensions={0} | all-to-all | bytes 655360 | tf_op jit(solution)/shard_map/all_to_all | solution.py:191
  110.2 0.0 collective-permute-start.1
  110.2 1.6 %collective-permute-done.1 = f32[640,128]{1,0:T(8,128)S(1)} collective-permute-done((f32[640,128]{1,0:T(8,128)S(1)}, f32[640,128]{1,0:T(8,128)S(1)}, u32[]{:S(2)}, u32[]{:S(2)}) %collective-permute-start.1) | collective-permute-done | bytes 327712 | tf_op jit(solution)/shard_map/ppermute | solution.py:185
  112.0 0.0 copy-done
  112.0 18.3 %factorize.1 = (f32[512,512]{1,0:T(8,128)S(1)}, f32[512,128]{1,0:T(8,128)S(1)}) custom-call(s32[1]{0:T(128)} %bitcast.core_ref, f32[1280,128]{1,0:T(8,128)S(1)} %pad_maximum_fusion.gram_ref, f32[512,128]{1,0:T(8,128)S(1)} %copy-done), custom_call_target="tpu_custom_call" | custom-call | tf_op jit(solution)/shard_map/factorize/pallas_call | solution.py:173
  130.2 1.7 %collective-permute-start.3 = (f32[512,128]{1,0:T(8,128)S(1)}, f32[512,128]{1,0:T(8,128)S(1)}, u32[]{:S(2)}, u32[]{:S(2)}) collective-permute-start(f32[512,128]{1,0:T(8,128)S(1)} %get-tuple-element.6), channel_id=1, source_target_pairs={{0,1},{1,0},{2,3},{3,2},{4,5},{5,4},{6,7},{7,6},{8,9},{9,8},{10,11... | collective-permute-start | bytes 786440 | tf_op jit(solution)/shard_map/ppermute | solution.py:185
  132.0 0.1 collective-permute-start.2
  132.1 1.1 collective-permute-done.3
  133.2 0.0 copy-start.1
  133.2 0.1 copy.11
  133.3 4.6 %fusion = f32[4,32,2048]{2,1,0:T(8,128)S(1)} fusion(f32[4,32,512]{2,1,0:T(8,128)S(1)} %bitcast.35, f32[512,2048,1]{1,0,2:T(8,128)} %bitcast.11), kind=kOutput, calls=%fused_computation.8 | convolution fusion | flops 1610612736 | bytes 5505024 | tf_op jit(solution)/shard_map/dot_general | solution.py:219
  137.9 18.4 %all_to_all.53 = f32[4,32,2048]{2,1,0:T(8,128)S(1)} all-to-all(f32[4,32,2048]{2,1,0:T(8,128)S(1)} %fusion), channel_id=1, replica_groups=mesh['mode'=4,'y'=4,'z'=8,'core'=2] {'mode'}, dimensions={0} | all-to-all | bytes 2097152 | tf_op jit(solution)/shard_map/all_to_all | solution.py:220
  156.3 1.1 copy.14
  157.3 0.0 copy-done.1
  157.3 0.0 collective-permute-done.2
  157.3 1.2 broadcast_select_fusion
  (9 shorter events, 0.3 us)
Async XLA Ops:
  5.3 52.2 %all-to-all-start = ((f32[128,4,2048]{2,0,1:T(8,128)}), f32[128,4,2048]{2,0,1:T(8,128)}, u32[]{:S(2)}, u32[]{:S(2)}) async-start(f32[128,4,2048]{2,0,1:T(8,128)} %bitcast.28), calls=%async_computation | async-start | bytes 8388608 | tf_op jit(solution)/shard_map/all_to_all | solution.py:213
  63.7 48.2 %copy-start = (f32[512,128]{1,0:T(8,128)S(1)}, f32[512,128]{1,0:T(8,128)}, u32[]{:S(2)}) copy-start(f32[512,128]{1,0:T(8,128)} %start_ref.1) | copy-start | bytes 786436
  63.8 1.7 %collective-permute-start = (f32[640,128]{1,0:T(8,128)S(1)}, f32[640,128]{1,0:T(8,128)S(1)}, u32[]{:S(2)}, u32[]{:S(2)}) collective-permute-start(f32[640,128]{1,0:T(8,128)S(1)} %dynamic-slice_bitcast_fusion), channel_id=1, source_target_pairs={{0,1},{1,0},{2,3},{3,2},{4,5},{5,4},{6,7},{7,6},{8,9},{9,8},{10,11... | collective-permute-start | bytes 983048 | tf_op jit(solution)/shard_map/ppermute | solution.py:185
  110.2 1.6 %collective-permute-start.1 = (f32[640,128]{1,0:T(8,128)S(1)}, f32[640,128]{1,0:T(8,128)S(1)}, u32[]{:S(2)}, u32[]{:S(2)}) collective-permute-start(f32[640,128]{1,0:T(8,128)S(1)} %bitcast.32), channel_id=1, source_target_pairs={{0,1},{1,0},{2,3},{3,2},{4,5},{5,4},{6,7},{7,6},{8,9},{9,8},{10,11... | collective-permute-start | bytes 983048 | tf_op jit(solution)/shard_map/ppermute | solution.py:185
  130.2 2.9 %collective-permute-start.3 = (f32[512,128]{1,0:T(8,128)S(1)}, f32[512,128]{1,0:T(8,128)S(1)}, u32[]{:S(2)}, u32[]{:S(2)}) collective-permute-start(f32[512,128]{1,0:T(8,128)S(1)} %get-tuple-element.6), channel_id=1, source_target_pairs={{0,1},{1,0},{2,3},{3,2},{4,5},{5,4},{6,7},{7,6},{8,9},{9,8},{10,11... | collective-permute-start | bytes 786440 | tf_op jit(solution)/shard_map/ppermute | solution.py:185
  132.0 25.4 %collective-permute-start.2 = (f32[512,512]{1,0:T(8,128)S(1)}, f32[512,512]{1,0:T(8,128)S(1)}, u32[]{:S(2)}, u32[]{:S(2)}) collective-permute-start(f32[512,512]{1,0:T(8,128)S(1)} %get-tuple-element.5), channel_id=1, source_target_pairs={{0,1},{1,0},{2,3},{3,2},{4,5},{5,4},{6,7},{7,6},{8,9},{9,8},{10,11... | collective-permute-start | bytes 3145736 | tf_op jit(solution)/shard_map/ppermute | solution.py:185
  133.2 24.2 %copy-start.1 = (f32[512,128]{1,0:T(8,128)}, f32[512,128]{1,0:T(8,128)S(1)}, u32[]{:S(2)}) copy-start(f32[512,128]{1,0:T(8,128)S(1)} %broadcast_select_fusion.3) | copy-start | bytes 786436

commit v2 on v1

v2 whole, which is shorter than its diff:
```python
import functools

import jax
import jax.numpy as jnp
from jax import lax
from jax.experimental import pallas as pl
from jax.experimental.pallas import tpu as pltpu
from jax.sharding import Mesh, PartitionSpec as P

ITERS = 3
MODE = 4
WIDTHS = (1024, 1024)
TILE = 512
HIGHEST = lax.Precision.HIGHEST
NB = 128
NT = (((1,), (1,)), ((), ()))
TN = (((0,), (0,)), ((), ()))
F32 = jnp.float32


def dot_exact(a, b, dims=(((1,), (0,)), ((), ()))):
    return lax.dot_general(a, b, dims, precision=HIGHEST, preferred_element_type=F32)


def cholesky_block(matrix, inverse_ref, upper_ref=None):
    n = matrix.shape[0]
    shape = (8, n)
    spread = functools.partial(jnp.broadcast_to, shape=shape)
    lane = lax.broadcasted_iota(jnp.int32, shape, 1)
    sub = lax.broadcasted_iota(jnp.int32, shape, 0)
    rows = [matrix[8 * i : 8 * i + 8, :] for i in range(n // 8)]
    for t in range(n // 8):
        first = 8 * t
        inside = (lane >= first) & (lane < first + 8)
        cols = {
            i: [spread(rows[i][:, first + j : first + j + 1]) for j in range(8)]
            for i in range(t, n // 8)
        }
        own = cols[t]
        top = rows[t]
        unit = jnp.where(lane == first + sub, 1.0, 0.0)
        recips = []
        mults = {i: [] for i in range(t + 1, n // 8)}
        for j in range(8):
            recip = 1.0 / spread(own[j][j : j + 1, :])
            recips.append(recip)
            mult = jnp.where(sub > j, own[j] * recip, 0.0)
            top = top - mult * spread(top[j : j + 1, :])
            unit = unit - mult * spread(unit[j : j + 1, :])
            pivot_row = {l: spread(own[l][j : j + 1, :]) for l in range(j + 1, 8)}
            for i in range(t + 1, n // 8):
                mult = cols[i][j] * recip
                mults[i].append(mult)
                for l in range(j + 1, 8):
                    cols[i][l] = cols[i][l] - mult * pivot_row[l]
            for l in range(j + 1, 8):
                own[l] = own[l] - (own[j] * pivot_row[l]) * recip
        scale = recips[0]
        for j in range(1, 8):
            scale = jnp.where(sub == j, recips[j], scale)
        scale = lax.rsqrt(1.0 / scale)
        inverse_ref[first : first + 8, :] = scale * jnp.where(lane < first, top, unit)
        if upper_ref is not None:
            upper_ref[first : first + 8, :] = jnp.where(lane >= first + sub, scale * top, 0.0)
        source = jnp.where(inside, unit, top)
        for i in range(t + 1, n // 8):
            left = jnp.where(inside, 0.0, rows[i])
            for j in range(8):
                left = left - mults[i][j] * spread(source[j : j + 1, :])
            rows[i] = left


def block_index(i, j):
    return i * (i + 1) // 2 + j


VMEM = pl.BlockSpec(memory_space=pltpu.VMEM)
SMEM = pl.BlockSpec(memory_space=pltpu.SMEM)
BF16 = jnp.bfloat16


def limit(mib):
    return pltpu.CompilerParams(vmem_limit_bytes=mib << 20)


def high_low(value):
    high = value.astype(BF16)
    return high, (value - high.astype(F32)).astype(BF16)


def gram_kernel(has_prior, final, place_ref, *refs):
    pieces, refs = refs[:MODE], refs[MODE:]
    prior_ref, refs = (refs[0], refs[1:]) if has_prior else (None, refs)
    wide_ref, outs, acc_ref = refs[0], refs[1:-1], refs[-1]
    m = acc_ref.shape[0]
    half = m // 2
    cols = pieces[0].shape[1]
    upper, lower, whole = slice(0, half), slice(half, m), slice(0, m)
    dot = functools.partial(lax.dot_general, dimension_numbers=NT, preferred_element_type=F32)
    for t in range(cols // TILE):
        for k, piece in enumerate(pieces):
            rows = pl.ds(pl.multiple_of(((place_ref[0] - k) & (MODE - 1)) * NB, NB), NB)
            high, low = high_low(piece[:, t * TILE : (t + 1) * TILE])
            wide_ref[rows, 2 * t * TILE : (2 * t + 1) * TILE] = high
            wide_ref[rows, (2 * t + 1) * TILE : (2 * t + 2) * TILE] = low

        def product(r, c):
            left = wide_ref[r, 2 * t * TILE : (2 * t + 2) * TILE]
            high = wide_ref[c, 2 * t * TILE : (2 * t + 1) * TILE]
            low = wide_ref[c, (2 * t + 1) * TILE : (2 * t + 2) * TILE]
            straight, turned = jnp.concatenate([high, low], axis=1), jnp.concatenate([low, high], axis=1)
            return dot(left, straight) + dot(left, turned)

        if t == 0:
            acc_ref[upper, upper] = product(upper, upper)
            acc_ref[lower, whole] = product(lower, whole)
        else:
            acc_ref[upper, upper] += product(upper, upper)
            acc_ref[lower, whole] += product(lower, whole)

    share = outs[0].shape[0] // NB

    def write(first, second):
        for i in range(m // NB):
            for j in range(i + 1):
                b = block_index(i, j)
                value = acc_ref[i * NB : (i + 1) * NB, j * NB : (j + 1) * NB]
                if prior_ref is not None:
                    value = value + prior_ref[b * NB : (b + 1) * NB, :]
                target = first if b < share else second
                target[b % share * NB : (b % share + 1) * NB, :] = value

    if final:
        pl.when(place_ref[1] == 0)(lambda: write(outs[0], outs[1]))
        pl.when(place_ref[1] != 0)(lambda: write(outs[1], outs[0]))
    else:
        write(outs[0], None)


def gram_lower(place, pieces, prior, final):
    rows, cols = pieces[0].shape
    m = rows * MODE
    rows_out = MODE * (MODE + 1) // 2 * NB
    priors = [] if prior is None else [prior]
    heights = [rows_out // 2] * 2 if final else [rows_out]
    return pl.pallas_call(
        functools.partial(gram_kernel, prior is not None, final),
        in_specs=[SMEM] + [VMEM] * (MODE + len(priors)),
        out_specs=[VMEM] * (1 + len(heights)),
        out_shape=[jax.ShapeDtypeStruct((m, 2 * cols), BF16)] + [jax.ShapeDtypeStruct((h, NB), F32) for h in heights],
        scratch_shapes=[pltpu.VMEM((m, m), F32)],
        compiler_params=limit(20),
        name="gram_lower",
    )(place, *pieces, *priors)


def core_kernel(place_ref, mine_ref, other_ref, wide_ref, *refs):
    outs, (result_ref, turned_ref) = refs[:MODE], refs[MODE:]
    r = mine_ref.shape[1]
    factor = jnp.where(place_ref[1] == 1, mine_ref[...], other_ref[...])
    turned_ref[:r, :], turned_ref[r:, :] = high_low(factor.T)
    for t in range(wide_ref.shape[1] // (2 * TILE)):
        both = jnp.dot(turned_ref[...], wide_ref[:, 2 * t * TILE : (2 * t + 2) * TILE], preferred_element_type=F32)
        big, small = both[:, :TILE], both[:, TILE:]
        result_ref[:, t * TILE : (t + 1) * TILE] = big[:r, :] + (big[r:, :] + (small[:r, :] + small[r:, :]))
    share = outs[0].shape[0]
    for k, out in enumerate(outs):
        at = pl.multiple_of(((place_ref[0] + k) & (MODE - 1)) * share, share)
        out[...] = result_ref[pl.ds(at, share), :]


def core_rows(place, mine, other, wide):
    m, r = mine.shape
    cols = wide.shape[1] // 2
    return pl.pallas_call(
        core_kernel,
        in_specs=[SMEM] + [VMEM] * 3,
        out_specs=[VMEM] * MODE,
        out_shape=[jax.ShapeDtypeStruct((r // MODE, cols), F32)] * MODE,
        scratch_shapes=[pltpu.VMEM((r, cols), F32), pltpu.VMEM((2 * r, m), BF16)],
        compiler_params=limit(16),
        name="core_rows",
    )(place, mine, other, wide)


def factor_kernel(scale, place_ref, mine_ref, other_ref, start_ref, tri_ref, basis_ref, full_ref, inv_ref, up_ref):
    m = full_ref.shape[0]
    nblk = m // NB

    def sl(i):
        return slice(i * NB, (i + 1) * NB)

    share = mine_ref.shape[0] // NB

    def block(halves, i, j):
        b = block_index(i, j)
        return halves[b // share][sl(b % share), :] * scale

    @pl.when(place_ref[1] == 0)
    def _():
        for i in range(nblk):
            for j in range(i + 1):
                full_ref[sl(i), sl(j)] = block((mine_ref, other_ref), i, j)

        def panel(p, carry):
            here = pl.ds(pl.multiple_of(p * NB, NB), NB)
            cholesky_block(full_ref[here, here], inv_ref, up_ref)
            column = dot_exact(full_ref[:, here], inv_ref[...], NT)
            row = lax.broadcasted_iota(jnp.int32, column.shape, 0)
            below = jnp.where(row >= (p + 1) * NB, column, 0.0)
            full_ref[:, here] = below

            @pl.when(p + 1 < nblk)
            def _():
                for j in range(1, nblk):
                    @pl.when(p < j)
                    def _():
                        full_ref[j * NB :, sl(j)] -= dot_exact(below[j * NB :, :], below[sl(j), :], NT)

            full_ref[here, here] = up_ref[...].T
            return carry

        lax.fori_loop(0, nblk, panel, 0)
        for i in range(nblk):
            for j in range(i + 1):
                tri_ref[sl(block_index(i, j)), :] = full_ref[sl(i), sl(j)]

    @pl.when(place_ref[1] != 0)
    def _():
        for i in range(nblk):
            for j in range(i + 1):
                b = block((other_ref, mine_ref), i, j)
                full_ref[sl(i), sl(j)] = b
                if j < i:
                    full_ref[sl(j), sl(i)] = b.T
        basis_ref[...] = start_ref[...]

        def step(_, carry):
            image = dot_exact(full_ref[...], basis_ref[...])
            cholesky_block(dot_exact(image, image, TN), inv_ref)
            basis_ref[...] = dot_exact(image, inv_ref[...], NT)
            return carry

        lax.fori_loop(0, ITERS, step, 0)


def factorize(place, mine, other, start_block, scale):
    m, r = start_block.shape
    packed = (2 * mine.shape[0], NB)
    return pl.pallas_call(
        functools.partial(factor_kernel, scale),
        in_specs=[SMEM, VMEM, VMEM, VMEM],
        out_specs=[VMEM, VMEM],
        out_shape=[jax.ShapeDtypeStruct(packed, F32), jax.ShapeDtypeStruct((m, r), F32)],
        scratch_shapes=[pltpu.VMEM((m, m), F32), pltpu.VMEM((NB, NB), F32), pltpu.VMEM((NB, NB), F32)],
        compiler_params=limit(24),
        name="factorize",
    )(place, mine, other, start_block)


def unpack_kernel(place_ref, mine_ref, other_ref, tri_ref):
    nblk = tri_ref.shape[0] // NB

    def fill(source):
        for i in range(nblk):
            for j in range(nblk):
                b = block_index(i, j)
                value = source[b * NB : (b + 1) * NB, :] if j <= i else jnp.zeros((NB, NB), F32)
                tri_ref[i * NB : (i + 1) * NB, j * NB : (j + 1) * NB] = value

    pl.when(place_ref[1] == 0)(lambda: fill(mine_ref))
    pl.when(place_ref[1] != 0)(lambda: fill(other_ref))


def unpack_triangle(place, mine, other):
    m = MODE * NB
    return pl.pallas_call(
        unpack_kernel,
        in_specs=[SMEM, VMEM, VMEM],
        out_specs=VMEM,
        out_shape=jax.ShapeDtypeStruct((m, m), F32),
        compiler_params=limit(16),
        name="unpack_triangle",
    )(place, mine, other)


def swap_cores(value):
    return lax.ppermute(value, "core", [(0, 1), (1, 0)])


def shift(value, axis, by):
    n = lax.axis_size(axis)
    return lax.ppermute(value, axis, [(i, (i + by) % n) for i in range(n)])


def spread_out(value, axes):
    n = lax.axis_size(axes)
    copies = jnp.broadcast_to(value[None], (n,) + value.shape)
    return lax.all_to_all(copies, axes, 0, 0, tiled=True)


def sum_z(value):
    value = value + lax.ppermute(value, "z", [(i, i ^ 1) for i in range(8)])
    side, back, other = (shift(value, "z", 2), shift(value, "z", 6), shift(value, "z", 4))
    return (value + other) + (side + back)


def sum_everywhere(mine, other):
    rows, lanes = mine.shape
    mine = mine + swap_cores(other)
    plane = ("mode", "y")
    n = lax.axis_size(plane)
    pieces = lax.all_to_all(mine.reshape(n, rows // n, lanes), plane, 0, 0, tiled=True)
    piece = sum_z(pieces.sum(0))
    mine = spread_out(piece, plane).reshape(rows, lanes)
    return mine, swap_cores(mine)


def per_device(unfolded, start_block):
    total_cols = unfolded.shape[1] * lax.axis_size(("y", "z", "core"))
    position, core_id = lax.axis_index("mode"), lax.axis_index("core")
    place = jnp.stack([position, core_id]).astype(jnp.int32)
    share = unfolded.shape[1] // MODE
    starts = [sum(WIDTHS[:c]) for c in range(len(WIDTHS))]

    def columns(source, k, c):
        owner = (position + k) & (MODE - 1)
        return lax.dynamic_slice_in_dim(source, owner * share + starts[c], WIDTHS[c], axis=1)

    received, source = [], unfolded
    for c in range(len(WIDTHS)):
        sent = {k: columns(source, k, c) for k in (2, 1, 3)}
        source, _ = lax.optimization_barrier((source, sent[2]))
        received.append([shift(sent[k], "mode", k) for k in range(1, MODE)])
    own = [columns(source, 0, c) for c in range(len(WIDTHS))]
    sums, wides = [None], []
    for c in range(len(WIDTHS)):
        wide, *sums = gram_lower(place, [own[c]] + received[c], sums[0], c == len(WIDTHS) - 1)
        wides.append(wide)
    sums = sum_everywhere(*sums)
    tri, basis = factorize(place, *sums, start_block, 1.0 / total_cols)
    basis_there = swap_cores(basis)
    factor = jnp.where(core_id == 1, basis, basis_there)
    triangle = unpack_triangle(place, tri, swap_cores(tri))
    landed = []
    for c, wide in enumerate(wides):
        parts = core_rows(place, basis, basis_there, wide)
        for k in (2, 1, 3, 0):
            got = shift(parts[k], "mode", k) if k else parts[0]
            landed.append((((position - k) & (MODE - 1)) * share + starts[c], got))
    core = jnp.zeros((factor.shape[1] // MODE, MODE * share), F32)
    core, triangle, factor, _ = lax.optimization_barrier((core, triangle, factor, parts[0]))
    for at, got in landed:
        core = lax.dynamic_update_slice_in_dim(core, got, at, axis=1)
    return (triangle, factor, core)


def solution(mesh):
    fine = Mesh(mesh.devices.reshape(4, 4, 8, 2), ("mode", "y", "z", "core"))
    rest = ("y", "z", "core")
    return jax.shard_map(
        per_device,
        mesh=fine,
        in_specs=(P("mode", rest), P()),
        out_specs=(P(), P(), P("mode", rest)),
        check_vma=False,
    )
```

time: 161 us -> 150 us (0.932); the launches traced: 159 us -> 149 us
  blocking collectives: 63 us -> 27 us
  starting transfers between devices: 8.93 us -> 28.7 us
  Pallas kernels: 24.5 us -> 31.1 us
  local copies, waits for them, and re-layouts: 5.93 us -> 11.3 us
  matrix products: 4.55 us -> 0 us
    all_to_all x1 -> x0, waiting for transfers between devices: 45.2 us -> none  [per_device(): lax.all_to_all(unfolded, 'mode', split_axis=1, concat_axis=0, tiled=True)]
    ppermute x0 -> x16, waiting for transfers between devices: none -> 44.1 us  [the longest x15 42.2 us: shift(): return lax.ppermute(value, axis, [(i, (i + by) % n) for i in range(n)])]
    ppermute x0 -> x16, starting transfers between devices: none -> 28.1 us  [the longest x15 26.1 us: shift(): return lax.ppermute(value, axis, [(i, (i + by) % n) for i in range(n)])]
    all_to_all x2 -> x1, blocking collectives: 33 us -> 14.7 us  [sum_everywhere(): lax.all_to_all(mine.reshape(n, rows // n, lanes), plane, 0, 0, tiled=True)]
    all_to_all x2 -> x1, blocking collectives: 30 us -> 12.3 us  [spread_out(): return lax.all_to_all(copies, axes, 0, 0, tiled=True)]
    all_to_all x1 -> x0, starting transfers between devices: 7.01 us -> none  [per_device(): lax.all_to_all(unfolded, 'mode', split_axis=1, concat_axis=0, tiled=True)]
    pallas_call x2 -> x6, Pallas kernels: 24.5 us -> 31.1 us  [the longest x1 20.1 us: factorize(): pl.pallas_call(functools.partial(factor_kernel, scale), in_specs=[SMEM, V...]
    unnamed x4 -> x12, local copies, waits for them, and re-layouts: 0.01 us -> 5.75 us
  transfers between devices with their start and end apart: 5 -> 20, of which waited for: 4 -> 13; matrix products, arithmetic and copies ran while one was open for 4% -> 3% of each run, Pallas kernels for 0% -> 5%
where the time goes in v2:
time: 150 us; the launch traced here: 149 us
  waiting for transfers between devices  49.3 us (33%)
  Pallas kernels  31.1 us (21%)
  starting transfers between devices  28.7 us (19%)
  blocking collectives  27 us (18%)
  local copies, waits for them, and re-layouts  11.3 us (8%)
    ppermute x15, waiting for transfers between devices, shift(): return lax.ppermute(value, axis, [(i, (i + by) % n) for i in range(n)])  42.2 us
    ppermute x15, starting transfers between devices, shift(): return lax.ppermute(value, axis, [(i, (i + by) % n) for i in range(n)])  26.1 us
    pallas_call x1, Pallas kernels, factorize(): pl.pallas_call(functools.partial(factor_kernel, scale), in_specs=[SMEM, V...  20.1 us
    all_to_all x1, blocking collectives, sum_everywhere(): lax.all_to_all(mine.reshape(n, rows // n, lanes), plane, 0, 0, tiled=True)  14.7 us
    all_to_all x1, blocking collectives, spread_out(): return lax.all_to_all(copies, axes, 0, 0, tiled=True)  12.3 us
    pallas_call x2, Pallas kernels, gram_lower(): pl.pallas_call(functools.partial(gram_kernel, prior is not None, final),...  6.21 us
    unnamed x12, local copies, waits for them, and re-layouts  5.75 us
    dynamic_slice x3, local copies, waits for them, and re-layouts, columns(): lax.dynamic_slice_in_dim(source, owner * share + starts[c], WIDTHS[c], ax...  5.38 us
  transfers between devices with their start and end apart: 20, of which 13 were waited for; matrix products, arithmetic and copies ran while one was open for 3% of the time, Pallas kernels for 5%

profile of v2, /device:TPU:6, one launch (start us, length us, event | category | flops | bytes accessed | tf_op | source)
XLA Modules:
  0.0 149.2 jit_solution(5133874233969540135)
XLA Ops:
  0.6 1.5 constant_dynamic-slice_fusion
  2.1 1.5 %collective-permute-start.4 = (f32[128,1024]{1,0:T(8,128)S(1)}, f32[128,1024]{1,0:T(8,128)S(1)}, u32[]{:S(2)}, u32[]{:S(2)}) collective-permute-start(f32[128,1024]{1,0:T(8,128)S(1)} %get-tuple-element.44), channel_id=1, source_target_pairs={{0,128},{64,192},{128,0},{192,64},{1,129},{65,193},{129,1},{193,65... | collective-permute-start | bytes 1572872 | tf_op jit(solution)/shard_map/ppermute | solution.py:293
  3.6 2.1 %collective-permute-start.3 = (f32[128,1024]{1,0:T(8,128)S(1)}, f32[128,1024]{1,0:T(8,128)S(1)}, u32[]{:S(2)}, u32[]{:S(2)}) collective-permute-start(f32[128,1024]{1,0:T(8,128)S(1)} %get-tuple-element.45), channel_id=1, source_target_pairs={{0,64},{64,128},{128,192},{192,0},{1,65},{65,129},{129,193},{193,1... | collective-permute-start | bytes 1572872 | tf_op jit(solution)/shard_map/ppermute | solution.py:293
  5.7 2.6 %constant_dynamic-slice_fusion.3 = (f32[128,1024]{1,0:T(8,128)}, f32[128,1024]{1,0:T(8,128)}, f32[128,1024]{1,0:T(8,128)}) fusion(f32[128,8192]{1,0:T(8,128)} %param.2, s32[]{:T(128)S(6)} %select_n.56, s32[]{:T(128)S(6)} %select_n.55, s32[]{:T(128)S(6)} %select_n.53), kind=kLoop, calls=%fused_computation.13 | loop fusion | bytes 3145740 | tf_op jit(solution)/shard_map/dynamic_slice | solution.py:328
  8.3 3.2 %collective-permute-start = (f32[128,1024]{1,0:T(8,128)}, f32[128,1024]{1,0:T(8,128)}, u32[]{:S(2)}, u32[]{:S(2)}) collective-permute-start(f32[128,1024]{1,0:T(8,128)} %get-tuple-element.49), channel_id=1, source_target_pairs={{0,64},{64,128},{128,192},{192,0},{1,65},{65,129},{129,193},{193,1... | collective-permute-start | bytes 1572872 | tf_op jit(solution)/shard_map/ppermute | solution.py:293
  11.5 0.4 collective-permute-start.1
  11.9 6.6 %collective-permute-done.4.refs_2_ = f32[128,1024]{1,0:T(8,128)S(1)} collective-permute-done((f32[128,1024]{1,0:T(8,128)S(1)}, f32[128,1024]{1,0:T(8,128)S(1)}, u32[]{:S(2)}, u32[]{:S(2)}) %collective-permute-start.4) | collective-permute-done | bytes 524320 | tf_op jit(solution)/shard_map/ppermute | solution.py:293
  18.6 0.8 collective-permute-start.2
  19.3 0.1 pad_add_fusion.place_ref
  19.4 1.3 constant_dynamic-slice_fusion.2
  20.8 8.6 %collective-permute-done.3.refs_1_ = f32[128,1024]{1,0:T(8,128)S(1)} collective-permute-done((f32[128,1024]{1,0:T(8,128)S(1)}, f32[128,1024]{1,0:T(8,128)S(1)}, u32[]{:S(2)}, u32[]{:S(2)}) %collective-permute-start.3) | collective-permute-done | bytes 524320 | tf_op jit(solution)/shard_map/ppermute | solution.py:293
  29.4 0.5 collective-permute-done.5.refs_3_
  29.9 0.8 copy-done.2
  30.7 1.0 copy-done.3
  31.7 2.7 %gram_lower.2 = (bf16[512,2048]{1,0:T(8,128)(2,1)S(1)}, f32[1280,128]{1,0:T(8,128)S(1)}) custom-call(s32[2]{0:T(128)S(1)} %pad_add_fusion.place_ref, f32[128,1024]{1,0:T(8,128)S(1)} %get-tuple-element.46.refs_0_, f32[128,1024]{1,0:T(8,128)S(1)} %collective-permute-done.3.refs_1_, f32[128,1024]{1,0:T(8,128)S(1)} %collective-permute-done.4.refs_2_, ...), custom_call_target="tpu_custom_call" | custom-call | tf_op jit(solution)/shard_map/gram_lower/pallas_call | solution.py:146
  34.4 6.3 %collective-permute-done.refs_1_ = f32[128,1024]{1,0:T(8,128)} collective-permute-done((f32[128,1024]{1,0:T(8,128)}, f32[128,1024]{1,0:T(8,128)}, u32[]{:S(2)}, u32[]{:S(2)}) %collective-permute-start) | collective-permute-done | bytes 524320 | tf_op jit(solution)/shard_map/ppermute | solution.py:293
  40.7 0.5 collective-permute-done.1.refs_2_
  41.2 10.0 %collective-permute-done.2.refs_3_ = f32[128,1024]{1,0:T(8,128)} collective-permute-done((f32[128,1024]{1,0:T(8,128)}, f32[128,1024]{1,0:T(8,128)}, u32[]{:S(2)}, u32[]{:S(2)}) %collective-permute-start.2) | collective-permute-done | bytes 524320 | tf_op jit(solution)/shard_map/ppermute | solution.py:293
  51.2 3.5 %gram_lower.3 = (bf16[512,2048]{1,0:T(8,128)(2,1)S(1)}, f32[640,128]{1,0:T(8,128)S(1)}, f32[640,128]{1,0:T(8,128)S(1)}) custom-call(s32[2]{0:T(128)S(1)} %pad_add_fusion.place_ref, f32[128,1024]{1,0:T(8,128)S(1)} %get-tuple-element.47.refs_0_, f32[128,1024]{1,0:T(8,128)} %collective-permute-done.refs_1_, f32[128,1024]{1,0:T(8,128)} %collective-permute-done.1.refs_2_, ...), custom_call_target="tpu_custom_call" | custom-call | tf_op jit(solution)/shard_map/gram_lower/pallas_call | solution.py:146
  54.7 1.3 copy-done
  56.1 1.6 %collective-permute-done.6 = f32[640,128]{1,0:T(8,128)S(1)} collective-permute-done((f32[640,128]{1,0:T(8,128)S(1)}, f32[640,128]{1,0:T(8,128)S(1)}, u32[]{:S(2)}, u32[]{:S(2)}) %collective-permute-start.6) | collective-permute-done | bytes 327712 | tf_op jit(solution)/shard_map/ppermute | solution.py:288
  57.7 14.7 %all_to_all.10 = f32[16,40,128]{2,1,0:T(8,128)S(1)} all-to-all(f32[16,40,128]{2,1,0:T(8,128)S(1)} %bitcast.6), channel_id=1, replica_groups=mesh['mode'=4,'y'=4,'z'=8,'core'=2] {'mode','y'}, dimensions={0} | all-to-all | bytes 655360 | tf_op jit(solution)/shard_map/all_to_all | solution.py:313
  72.5 2.0 %collective-permute-start.7 = (f32[40,128]{1,0:T(8,128)S(1)}, f32[40,128]{1,0:T(8,128)S(1)}, u32[]{:S(2)}, u32[]{:S(2)}) collective-permute-start(f32[40,128]{1,0:T(8,128)S(1)} %reduce_sum.9), channel_id=1, source_target_pairs={{0,2},{2,0},{4,6},{6,4},{8,10},{10,8},{12,14},{14,12},{1,3},{3,1},... | collective-permute-start | bytes 61448 | tf_op jit(solution)/shard_map/ppermute | solution.py:303
  74.5 1.9 %collective-permute-done.7 = f32[40,128]{1,0:T(8,128)S(1)} collective-permute-done((f32[40,128]{1,0:T(8,128)S(1)}, f32[40,128]{1,0:T(8,128)S(1)}, u32[]{:S(2)}, u32[]{:S(2)}) %collective-permute-start.7) | collective-permute-done | bytes 20512 | tf_op jit(solution)/shard_map/ppermute | solution.py:303
  76.3 6.3 %collective-permute-start.10 = (f32[40,128]{1,0:T(8,128)S(1)}, f32[40,128]{1,0:T(8,128)S(1)}, u32[]{:S(2)}, u32[]{:S(2)}) collective-permute-start(f32[40,128]{1,0:T(8,128)S(1)} %add.126), channel_id=1, source_target_pairs={{0,12},{2,14},{4,0},{6,2},{8,4},{10,6},{12,8},{14,10},{1,13},{3,15... | collective-permute-start | bytes 61448 | tf_op jit(solution)/shard_map/ppermute | solution.py:293
  82.6 1.1 collective-permute-start.8
  83.7 2.8 %collective-permute-start.9 = (f32[40,128]{1,0:T(8,128)S(1)}, f32[40,128]{1,0:T(8,128)S(1)}, u32[]{:S(2)}, u32[]{:S(2)}) collective-permute-start(f32[40,128]{1,0:T(8,128)S(1)} %add.126), channel_id=1, source_target_pairs={{0,4},{2,6},{4,8},{6,10},{8,12},{10,14},{12,0},{14,2},{1,5},{3,7},... | collective-permute-start | bytes 61448 | tf_op jit(solution)/shard_map/ppermute | solution.py:293
  86.5 3.8 %collective-permute-done.8 = f32[40,128]{1,0:T(8,128)S(1)} collective-permute-done((f32[40,128]{1,0:T(8,128)S(1)}, f32[40,128]{1,0:T(8,128)S(1)}, u32[]{:S(2)}, u32[]{:S(2)}) %collective-permute-start.8) | collective-permute-done | bytes 20512 | tf_op jit(solution)/shard_map/ppermute | solution.py:293
  90.4 12.3 %all_to_all.11 = f32[16,40,128]{2,1,0:T(8,128)S(1)} all-to-all(f32[16,40,128]{2,1,0:T(8,128)S(1)} %broadcast_in_dim.10), channel_id=1, replica_groups=mesh['mode'=4,'y'=4,'z'=8,'core'=2] {'mode','y'}, dimensions={0} | all-to-all | bytes 655360 | tf_op jit(solution)/shard_map/all_to_all | solution.py:299
  102.7 1.6 %collective-permute-done.11.other_ref = f32[640,128]{1,0:T(8,128)S(1)} collective-permute-done((f32[640,128]{1,0:T(8,128)S(1)}, f32[640,128]{1,0:T(8,128)S(1)}, u32[]{:S(2)}, u32[]{:S(2)}) %collective-permute-start.11) | collective-permute-done | bytes 327712 | tf_op jit(solution)/shard_map/ppermute | solution.py:288
  104.3 20.1 %factorize.1 = (f32[1280,128]{1,0:T(8,128)S(1)}, f32[512,128]{1,0:T(8,128)S(1)}) custom-call(s32[2]{0:T(128)S(1)} %pad_add_fusion.place_ref, f32[640,128]{1,0:T(8,128)S(1)} %bitcast.5, f32[640,128]{1,0:T(8,128)S(1)} %collective-permute-done.11.other_ref, f32[512,128]{1,0:T(8,128)S(1)} %copy-done.4), custom_call_target="tpu_custom_call" | custom-call | tf_op jit(solution)/shard_map/factorize/pallas_call | solution.py:250
  124.4 0.2 collective-permute-start.12
  124.6 0.4 collective-permute-start.13
  125.0 2.0 %collective-permute-done.13.other_ref = f32[512,128]{1,0:T(8,128)S(1)} collective-permute-done((f32[512,128]{1,0:T(8,128)S(1)}, f32[512,128]{1,0:T(8,128)S(1)}, u32[]{:S(2)}, u32[]{:S(2)}) %collective-permute-start.13) | collective-permute-done | bytes 262176 | tf_op jit(solution)/shard_map/ppermute | solution.py:288
  127.0 1.3 core_rows.3
  128.3 1.8 %collective-permute-start.14 = (f32[32,1024]{1,0:T(8,128)S(1)}, f32[32,1024]{1,0:T(8,128)S(1)}, u32[]{:S(2)}, u32[]{:S(2)}) collective-permute-start(f32[32,1024]{1,0:T(8,128)S(1)} %get-tuple-element.36), channel_id=1, source_target_pairs={{0,128},{64,192},{128,0},{192,64},{1,129},{65,193},{129,1},{193,65... | collective-permute-start | bytes 393224 | tf_op jit(solution)/shard_map/ppermute | solution.py:293
  130.1 1.7 %collective-permute-start.15 = (f32[32,1024]{1,0:T(8,128)S(1)}, f32[32,1024]{1,0:T(8,128)S(1)}, u32[]{:S(2)}, u32[]{:S(2)}) collective-permute-start(f32[32,1024]{1,0:T(8,128)S(1)} %get-tuple-element.37), channel_id=1, source_target_pairs={{0,64},{64,128},{128,192},{192,0},{1,65},{65,129},{129,193},{193,1... | collective-permute-start | bytes 393224 | tf_op jit(solution)/shard_map/ppermute | solution.py:293
  131.8 0.3 collective-permute-start.16
  132.1 1.6 %copy-done.1 = bf16[512,2048]{1,0:T(8,128)(2,1)S(1)} copy-done((bf16[512,2048]{1,0:T(8,128)(2,1)S(1)}, bf16[512,2048]{1,0:T(8,128)(2,1)}, u32[]{:S(2)}) %copy-start.1) | copy-done | bytes 2097176
  133.7 1.3 core_rows.2
  135.0 1.9 %collective-permute-start.17 = (f32[32,1024]{1,0:T(8,128)S(1)}, f32[32,1024]{1,0:T(8,128)S(1)}, u32[]{:S(2)}, u32[]{:S(2)}) collective-permute-start(f32[32,1024]{1,0:T(8,128)S(1)} %get-tuple-element.40), channel_id=1, source_target_pairs={{0,128},{64,192},{128,0},{192,64},{1,129},{65,193},{129,1},{193,65... | collective-permute-start | bytes 393224 | tf_op jit(solution)/shard_map/ppermute | solution.py:293
  137.0 0.7 broadcast_select_fusion
  137.7 2.1 %collective-permute-start.18 = (f32[32,1024]{1,0:T(8,128)S(1)}, f32[32,1024]{1,0:T(8,128)S(1)}, u32[]{:S(2)}, u32[]{:S(2)}) collective-permute-start(f32[32,1024]{1,0:T(8,128)S(1)} %get-tuple-element.41), channel_id=1, source_target_pairs={{0,64},{64,128},{128,192},{192,0},{1,65},{65,129},{129,193},{193,1... | collective-permute-start | bytes 393224 | tf_op jit(solution)/shard_map/ppermute | solution.py:293
  139.8 2.2 %unpack_triangle.1 = f32[512,512]{1,0:T(8,128)} custom-call(s32[2]{0:T(128)S(1)} %pad_add_fusion.place_ref, f32[1280,128]{1,0:T(8,128)S(1)} %get-tuple-element.28.mine_ref, f32[1280,128]{1,0:T(8,128)} %collective-permute-done.12.other_ref), custom_call_target="tpu_custom_call" | custom-call | tf_op jit(solution)/shard_map/unpack_triangle/pallas_call | solution.py:277
  142.0 0.1 broadcast_in_dim.4
  142.2 2.2 %collective-permute-done.18 = f32[32,1024]{1,0:T(8,128)S(1)} collective-permute-done((f32[32,1024]{1,0:T(8,128)S(1)}, f32[32,1024]{1,0:T(8,128)S(1)}, u32[]{:S(2)}, u32[]{:S(2)}) %collective-permute-start.18) | collective-permute-done | bytes 131104 | tf_op jit(solution)/shard_map/ppermute | solution.py:293
  144.4 3.8 %collective-permute-done.19 = f32[32,1024]{1,0:T(8,128)S(1)} collective-permute-done((f32[32,1024]{1,0:T(8,128)S(1)}, f32[32,1024]{1,0:T(8,128)S(1)}, u32[]{:S(2)}, u32[]{:S(2)}) %collective-permute-start.19) | collective-permute-done | bytes 131104 | tf_op jit(solution)/shard_map/ppermute | solution.py:293
  148.2 1.0 copy-done.5
  (31 shorter events, 0.3 us)
Async XLA Ops:
  2.1 16.4 %collective-permute-start.4 = (f32[128,1024]{1,0:T(8,128)S(1)}, f32[128,1024]{1,0:T(8,128)S(1)}, u32[]{:S(2)}, u32[]{:S(2)}) collective-permute-start(f32[128,1024]{1,0:T(8,128)S(1)} %get-tuple-element.44), channel_id=1, source_target_pairs={{0,128},{64,192},{128,0},{192,64},{1,129},{65,193},{129,1},{193,65... | collective-permute-start | bytes 1572872 | tf_op jit(solution)/shard_map/ppermute | solution.py:293
  3.6 25.8 %collective-permute-start.3 = (f32[128,1024]{1,0:T(8,128)S(1)}, f32[128,1024]{1,0:T(8,128)S(1)}, u32[]{:S(2)}, u32[]{:S(2)}) collective-permute-start(f32[128,1024]{1,0:T(8,128)S(1)} %get-tuple-element.45), channel_id=1, source_target_pairs={{0,64},{64,128},{128,192},{192,0},{1,65},{65,129},{129,193},{193,1... | collective-permute-start | bytes 1572872 | tf_op jit(solution)/shard_map/ppermute | solution.py:293
  5.7 24.2 %collective-permute-start.5 = (f32[128,1024]{1,0:T(8,128)S(1)}, f32[128,1024]{1,0:T(8,128)S(1)}, u32[]{:S(2)}, u32[]{:S(2)}) collective-permute-start(f32[128,1024]{1,0:T(8,128)S(1)} %get-tuple-element.43), channel_id=1, source_target_pairs={{0,192},{64,0},{128,64},{192,128},{1,193},{65,1},{129,65},{193,129... | collective-permute-start | bytes 1572872 | tf_op jit(solution)/shard_map/ppermute | solution.py:293
  8.3 32.5 %collective-permute-start = (f32[128,1024]{1,0:T(8,128)}, f32[128,1024]{1,0:T(8,128)}, u32[]{:S(2)}, u32[]{:S(2)}) collective-permute-start(f32[128,1024]{1,0:T(8,128)} %get-tuple-element.49), channel_id=1, source_target_pairs={{0,64},{64,128},{128,192},{192,0},{1,65},{65,129},{129,193},{193,1... | collective-permute-start | bytes 1572872 | tf_op jit(solution)/shard_map/ppermute | solution.py:293
  11.5 29.7 %collective-permute-start.1 = (f32[128,1024]{1,0:T(8,128)}, f32[128,1024]{1,0:T(8,128)}, u32[]{:S(2)}, u32[]{:S(2)}) collective-permute-start(f32[128,1024]{1,0:T(8,128)} %get-tuple-element.50), channel_id=1, source_target_pairs={{0,128},{64,192},{128,0},{192,64},{1,129},{65,193},{129,1},{193,65... | collective-permute-start | bytes 1572872 | tf_op jit(solution)/shard_map/ppermute | solution.py:293
  18.6 32.6 %collective-permute-start.2 = (f32[128,1024]{1,0:T(8,128)}, f32[128,1024]{1,0:T(8,128)}, u32[]{:S(2)}, u32[]{:S(2)}) collective-permute-start(f32[128,1024]{1,0:T(8,128)} %get-tuple-element.48), channel_id=1, source_target_pairs={{0,192},{64,0},{128,64},{192,128},{1,193},{65,1},{129,65},{193,129... | collective-permute-start | bytes 1572872 | tf_op jit(solution)/shard_map/ppermute | solution.py:293
  19.4 84.9 %copy-start.4 = (f32[512,128]{1,0:T(8,128)S(1)}, f32[512,128]{1,0:T(8,128)}, u32[]{:S(2)}) copy-start(f32[512,128]{1,0:T(8,128)} %start_ref.1) | copy-start | bytes 786436
  29.9 0.8 copy-start.2
  30.7 1.0 copy-start.3
  54.7 1.3 copy-start
  56.1 1.6 %collective-permute-start.6 = (f32[640,128]{1,0:T(8,128)S(1)}, f32[640,128]{1,0:T(8,128)S(1)}, u32[]{:S(2)}, u32[]{:S(2)}) collective-permute-start(f32[640,128]{1,0:T(8,128)S(1)} %get-tuple-element.27), channel_id=1, source_target_pairs={{0,1},{1,0},{2,3},{3,2},{4,5},{5,4},{6,7},{7,6},{8,9},{9,8},{10,11... | collective-permute-start | bytes 983048 | tf_op jit(solution)/shard_map/ppermute | solution.py:288
  72.5 3.9 %collective-permute-start.7 = (f32[40,128]{1,0:T(8,128)S(1)}, f32[40,128]{1,0:T(8,128)S(1)}, u32[]{:S(2)}, u32[]{:S(2)}) collective-permute-start(f32[40,128]{1,0:T(8,128)S(1)} %reduce_sum.9), channel_id=1, source_target_pairs={{0,2},{2,0},{4,6},{6,4},{8,10},{10,8},{12,14},{14,12},{1,3},{3,1},... | collective-permute-start | bytes 61448 | tf_op jit(solution)/shard_map/ppermute | solution.py:303
  76.3 10.2 %collective-permute-start.10 = (f32[40,128]{1,0:T(8,128)S(1)}, f32[40,128]{1,0:T(8,128)S(1)}, u32[]{:S(2)}, u32[]{:S(2)}) collective-permute-start(f32[40,128]{1,0:T(8,128)S(1)} %add.126), channel_id=1, source_target_pairs={{0,12},{2,14},{4,0},{6,2},{8,4},{10,6},{12,8},{14,10},{1,13},{3,15... | collective-permute-start | bytes 61448 | tf_op jit(solution)/shard_map/ppermute | solution.py:293
  82.6 7.7 %collective-permute-start.8 = (f32[40,128]{1,0:T(8,128)S(1)}, f32[40,128]{1,0:T(8,128)S(1)}, u32[]{:S(2)}, u32[]{:S(2)}) collective-permute-start(f32[40,128]{1,0:T(8,128)S(1)} %add.126), channel_id=1, source_target_pairs={{0,8},{2,10},{4,12},{6,14},{8,0},{10,2},{12,4},{14,6},{1,9},{3,11}... | collective-permute-start | bytes 61448 | tf_op jit(solution)/shard_map/ppermute | solution.py:293
  83.7 6.6 %collective-permute-start.9 = (f32[40,128]{1,0:T(8,128)S(1)}, f32[40,128]{1,0:T(8,128)S(1)}, u32[]{:S(2)}, u32[]{:S(2)}) collective-permute-start(f32[40,128]{1,0:T(8,128)S(1)} %add.126), channel_id=1, source_target_pairs={{0,4},{2,6},{4,8},{6,10},{8,12},{10,14},{12,0},{14,2},{1,5},{3,7},... | collective-permute-start | bytes 61448 | tf_op jit(solution)/shard_map/ppermute | solution.py:293
  102.7 1.6 %collective-permute-start.11 = (f32[640,128]{1,0:T(8,128)S(1)}, f32[640,128]{1,0:T(8,128)S(1)}, u32[]{:S(2)}, u32[]{:S(2)}) collective-permute-start(f32[640,128]{1,0:T(8,128)S(1)} %bitcast.4), channel_id=1, source_target_pairs={{0,1},{1,0},{2,3},{3,2},{4,5},{5,4},{6,7},{7,6},{8,9},{9,8},{10,11... | collective-permute-start | bytes 983048 | tf_op jit(solution)/shard_map/ppermute | solution.py:288
  124.4 13.3 %collective-permute-start.12 = (f32[1280,128]{1,0:T(8,128)S(1)}, f32[1280,128]{1,0:T(8,128)}, u32[]{:S(2)}, u32[]{:S(2)}) collective-permute-start(f32[1280,128]{1,0:T(8,128)S(1)} %get-tuple-element.28.mine_ref), channel_id=1, source_target_pairs={{0,1},{1,0},{2,3},{3,2},{4,5},{5,4},{6,7},{7,6},{8,9},{9,8},{10,11... | collective-permute-start | bytes 1966088 | tf_op jit(solution)/shard_map/ppermute | solution.py:288
  124.6 2.3 %collective-permute-start.13 = (f32[512,128]{1,0:T(8,128)S(1)}, f32[512,128]{1,0:T(8,128)S(1)}, u32[]{:S(2)}, u32[]{:S(2)}) collective-permute-start(f32[512,128]{1,0:T(8,128)S(1)} %get-tuple-element.29.mine_ref), channel_id=1, source_target_pairs={{0,1},{1,0},{2,3},{3,2},{4,5},{5,4},{6,7},{7,6},{8,9},{9,8},{10,11... | collective-permute-start | bytes 786440 | tf_op jit(solution)/shard_map/ppermute | solution.py:288
  128.3 13.7 %collective-permute-start.14 = (f32[32,1024]{1,0:T(8,128)S(1)}, f32[32,1024]{1,0:T(8,128)S(1)}, u32[]{:S(2)}, u32[]{:S(2)}) collective-permute-start(f32[32,1024]{1,0:T(8,128)S(1)} %get-tuple-element.36), channel_id=1, source_target_pairs={{0,128},{64,192},{128,0},{192,64},{1,129},{65,193},{129,1},{193,65... | collective-permute-start | bytes 393224 | tf_op jit(solution)/shard_map/ppermute | solution.py:293
  130.1 12.0 %collective-permute-start.15 = (f32[32,1024]{1,0:T(8,128)S(1)}, f32[32,1024]{1,0:T(8,128)S(1)}, u32[]{:S(2)}, u32[]{:S(2)}) collective-permute-start(f32[32,1024]{1,0:T(8,128)S(1)} %get-tuple-element.37), channel_id=1, source_target_pairs={{0,64},{64,128},{128,192},{192,0},{1,65},{65,129},{129,193},{193,1... | collective-permute-start | bytes 393224 | tf_op jit(solution)/shard_map/ppermute | solution.py:293
  131.8 10.3 %collective-permute-start.16 = (f32[32,1024]{1,0:T(8,128)S(1)}, f32[32,1024]{1,0:T(8,128)S(1)}, u32[]{:S(2)}, u32[]{:S(2)}) collective-permute-start(f32[32,1024]{1,0:T(8,128)S(1)} %get-tuple-element.38), channel_id=1, source_target_pairs={{0,192},{64,0},{128,64},{192,128},{1,193},{65,1},{129,65},{193,129... | collective-permute-start | bytes 393224 | tf_op jit(solution)/shard_map/ppermute | solution.py:293
  132.1 1.6 %copy-start.1 = (bf16[512,2048]{1,0:T(8,128)(2,1)S(1)}, bf16[512,2048]{1,0:T(8,128)(2,1)}, u32[]{:S(2)}) copy-start(bf16[512,2048]{1,0:T(8,128)(2,1)} %copy-done) | copy-start | bytes 6291460
  135.0 7.2 %collective-permute-start.17 = (f32[32,1024]{1,0:T(8,128)S(1)}, f32[32,1024]{1,0:T(8,128)S(1)}, u32[]{:S(2)}, u32[]{:S(2)}) collective-permute-start(f32[32,1024]{1,0:T(8,128)S(1)} %get-tuple-element.40), channel_id=1, source_target_pairs={{0,128},{64,192},{128,0},{192,64},{1,129},{65,193},{129,1},{193,65... | collective-permute-start | bytes 393224 | tf_op jit(solution)/shard_map/ppermute | solution.py:293
  137.7 6.7 %collective-permute-start.18 = (f32[32,1024]{1,0:T(8,128)S(1)}, f32[32,1024]{1,0:T(8,128)S(1)}, u32[]{:S(2)}, u32[]{:S(2)}) collective-permute-start(f32[32,1024]{1,0:T(8,128)S(1)} %get-tuple-element.41), channel_id=1, source_target_pairs={{0,64},{64,128},{128,192},{192,0},{1,65},{65,129},{129,193},{193,1... | collective-permute-start | bytes 393224 | tf_op jit(solution)/shard_map/ppermute | solution.py:293
  142.0 6.2 %collective-permute-start.19 = (f32[32,1024]{1,0:T(8,128)S(1)}, f32[32,1024]{1,0:T(8,128)S(1)}, u32[]{:S(2)}, u32[]{:S(2)}) collective-permute-start(f32[32,1024]{1,0:T(8,128)S(1)} %get-tuple-element.42), channel_id=1, source_target_pairs={{0,192},{64,0},{128,64},{192,128},{1,193},{65,1},{129,65},{193,129... | collective-permute-start | bytes 393224 | tf_op jit(solution)/shard_map/ppermute | solution.py:293
  148.2 1.0 copy-start.5

commit v3 on v2

--- a/solution.py
+++ b/solution.py
@@ -77,6 +77,7 @@
 VMEM = pl.BlockSpec(memory_space=pltpu.VMEM)
 SMEM = pl.BlockSpec(memory_space=pltpu.SMEM)
 BF16 = jnp.bfloat16
+NO_COST = pl.CostEstimate(flops=0, transcendentals=0, bytes_accessed=0)
 
 
 def limit(mib):
@@ -86,6 +87,32 @@
 def high_low(value):
     high = value.astype(BF16)
     return high, (value - high.astype(F32)).astype(BF16)
+
+
+def slice_kernel(shifts, start, share, place_ref, source_ref, *refs):
+    outs, sem = refs[:-1], refs[-1]
+    width = outs[0].shape[1]
+    copies = []
+    for n, k in enumerate(shifts):
+        at = pl.multiple_of(((place_ref[0] + k) & (MODE - 1)) * share + start, NB)
+        copies.append(pltpu.make_async_copy(source_ref.at[:, pl.ds(at, width)], outs[n], sem.at[n]))
+        copies[-1].start()
+    for copy in copies:
+        copy.wait()
+
+
+def column_slices(place, source, shifts, start, width):
+    rows, cols = source.shape
+    return pl.pallas_call(
+        functools.partial(slice_kernel, shifts, start, cols // MODE),
+        in_specs=[SMEM, pl.BlockSpec(memory_space=pl.ANY)],
+        out_specs=[VMEM] * len(shifts),
+        out_shape=[jax.ShapeDtypeStruct((rows, width), F32)] * len(shifts),
+        scratch_shapes=[pltpu.SemaphoreType.DMA((len(shifts),))],
+        compiler_params=limit(4),
+        cost_estimate=NO_COST,
+        name="column_slices",
+    )(place, source)
 
 
 def gram_kernel(has_prior, final, place_ref, *refs):
@@ -149,7 +176,8 @@
         out_specs=[VMEM] * (1 + len(heights)),
         out_shape=[jax.ShapeDtypeStruct((m, 2 * cols), BF16)] + [jax.ShapeDtypeStruct((h, NB), F32) for h in heights],
         scratch_shapes=[pltpu.VMEM((m, m), F32)],
-        compiler_params=limit(20),
+        compiler_params=limit(8),
+        cost_estimate=NO_COST,
         name="gram_lower",
     )(place, *pieces, *priors)
 
@@ -178,7 +206,8 @@
         out_specs=[VMEM] * MODE,
         out_shape=[jax.ShapeDtypeStruct((r // MODE, cols), F32)] * MODE,
         scratch_shapes=[pltpu.VMEM((r, cols), F32), pltpu.VMEM((2 * r, m), BF16)],
-        compiler_params=limit(16),
+        compiler_params=limit(6),
+        cost_estimate=NO_COST,
         name="core_rows",
     )(place, mine, other, wide)
 
@@ -253,7 +282,8 @@
         out_specs=[VMEM, VMEM],
         out_shape=[jax.ShapeDtypeStruct(packed, F32), jax.ShapeDtypeStruct((m, r), F32)],
         scratch_shapes=[pltpu.VMEM((m, m), F32), pltpu.VMEM((NB, NB), F32), pltpu.VMEM((NB, NB), F32)],
-        compiler_params=limit(24),
+        compiler_params=limit(8),
+        cost_estimate=NO_COST,
         name="factorize",
     )(place, mine, other, start_block)
 
@@ -279,7 +309,8 @@
         in_specs=[SMEM, VMEM, VMEM],
         out_specs=VMEM,
         out_shape=jax.ShapeDtypeStruct((m, m), F32),
-        compiler_params=limit(16),
+        compiler_params=limit(4),
+        cost_estimate=NO_COST,
         name="unpack_triangle",
     )(place, mine, other)
 
@@ -323,16 +354,19 @@
     share = unfolded.shape[1] // MODE
     starts = [sum(WIDTHS[:c]) for c in range(len(WIDTHS))]
 
-    def columns(source, k, c):
-        owner = (position + k) & (MODE - 1)
-        return lax.dynamic_slice_in_dim(source, owner * share + starts[c], WIDTHS[c], axis=1)
+    def columns(k, width):
+        owner = ((position + k) & (MODE - 1)).astype(jnp.uint32)
+        return lax.dynamic_slice_in_dim(unfolded, owner * share, width, axis=1)
 
     received, source = [], unfolded
-    for c in range(len(WIDTHS)):
-        sent = {k: columns(source, k, c) for k in (2, 1, 3)}
+    for start, width in zip(starts, WIDTHS):
+        if start == 0:
+            sent = {k: columns(k, width) for k in (2, 1, 3)}
+        else:
+            sent = dict(zip((2, 1, 3), column_slices(place, source, (2, 1, 3), start, width)))
         source, _ = lax.optimization_barrier((source, sent[2]))
         received.append([shift(sent[k], "mode", k) for k in range(1, MODE)])
-    own = [columns(source, 0, c) for c in range(len(WIDTHS))]
+    own = [column_slices(place, source, (0,), start, width)[0] for start, width in zip(starts, WIDTHS)]
     sums, wides = [None], []
     for c in range(len(WIDTHS)):
         wide, *sums = gram_lower(place, [own[c]] + received[c], sums[0], c == len(WIDTHS) - 1)

time: 150 us -> 148 us (0.987)
  local copies, waits for them, and re-layouts: 11.3 us -> 9.61 us
    dynamic_slice x3 -> x1, local copies, waits for them, and re-layouts: 5.38 us -> 1.47 us  [columns(): return lax.dynamic_slice_in_dim(unfolded, owner * share, width, axis=1)]
    unnamed x12 -> x14, local copies, waits for them, and re-layouts: 5.75 us -> 7.92 us
    pallas_call x0 -> x3, Pallas kernels: none -> 1.88 us  [column_slices(): pl.pallas_call(functools.partial(slice_kernel, shifts, start, cols // MOD...]
  transfers between devices with their start and end apart: 20 -> 20, of which waited for: 13 -> 13; matrix products, arithmetic and copies ran while one was open for 3% -> 1% of each run, Pallas kernels for 5% -> 6%
where the time goes in v3:
time: 148 us
  waiting for transfers between devices  48.3 us (33%)
  Pallas kernels  32.2 us (22%)
  starting transfers between devices  29.4 us (20%)
  blocking collectives  26.7 us (18%)
  local copies, waits for them, and re-layouts  9.61 us (6%)
    ppermute x15, waiting for transfers between devices, shift(): return lax.ppermute(value, axis, [(i, (i + by) % n) for i in range(n)])  41.3 us
    ppermute x15, starting transfers between devices, shift(): return lax.ppermute(value, axis, [(i, (i + by) % n) for i in range(n)])  26.8 us
    pallas_call x1, Pallas kernels, factorize(): pl.pallas_call(functools.partial(factor_kernel, scale), in_specs=[SMEM, V...  20.1 us
    all_to_all x1, blocking collectives, sum_everywhere(): lax.all_to_all(mine.reshape(n, rows // n, lanes), plane, 0, 0, tiled=True)  14.4 us
    all_to_all x1, blocking collectives, spread_out(): return lax.all_to_all(copies, axes, 0, 0, tiled=True)  12.3 us
    unnamed x14, local copies, waits for them, and re-layouts  7.92 us
    pallas_call x2, Pallas kernels, gram_lower(): pl.pallas_call(functools.partial(gram_kernel, prior is not None, final),...  5.39 us
    ppermute x4, waiting for transfers between devices, swap_cores(): return lax.ppermute(value, 'core', [(0, 1), (1, 0)])  5.19 us
  transfers between devices with their start and end apart: 20, of which 13 were waited for; matrix products, arithmetic and copies ran while one was open for 1% of the time, Pallas kernels for 6%

profile of v3, /device:TPU:6, one launch (start us, length us, event | category | flops | bytes accessed | tf_op | source)
XLA Modules:
  0.0 148.0 jit_solution(6723926985990985867)
XLA Ops:
  0.6 1.5 constant_dynamic-slice_fusion
  2.1 1.5 %collective-permute-start.4 = (f32[128,1024]{1,0:T(8,128)S(1)}, f32[128,1024]{1,0:T(8,128)S(1)}, u32[]{:S(2)}, u32[]{:S(2)}) collective-permute-start(f32[128,1024]{1,0:T(8,128)S(1)} %get-tuple-element.50), channel_id=1, source_target_pairs={{0,128},{64,192},{128,0},{192,64},{1,129},{65,193},{129,1},{193,65... | collective-permute-start | bytes 1572872 | tf_op jit(solution)/shard_map/ppermute | solution.py:324
  3.6 2.1 %collective-permute-start.3 = (f32[128,1024]{1,0:T(8,128)S(1)}, f32[128,1024]{1,0:T(8,128)S(1)}, u32[]{:S(2)}, u32[]{:S(2)}) collective-permute-start(f32[128,1024]{1,0:T(8,128)S(1)} %get-tuple-element.51), channel_id=1, source_target_pairs={{0,64},{64,128},{128,192},{192,0},{1,65},{65,129},{129,193},{193,1... | collective-permute-start | bytes 1572872 | tf_op jit(solution)/shard_map/ppermute | solution.py:324
  5.8 2.2 %copy-done = f32[128,8192]{1,0:T(8,128)S(1)} copy-done((f32[128,8192]{1,0:T(8,128)S(1)}, f32[128,8192]{1,0:T(8,128)}, u32[]{:S(2)}) %copy-start) | copy-done | bytes 4194328
  8.0 0.7 column_slices.3
  8.7 2.1 %collective-permute-start.1 = (f32[128,1024]{1,0:T(8,128)S(1)}, f32[128,1024]{1,0:T(8,128)S(1)}, u32[]{:S(2)}, u32[]{:S(2)}) collective-permute-start(f32[128,1024]{1,0:T(8,128)S(1)} %get-tuple-element.27), channel_id=1, source_target_pairs={{0,128},{64,192},{128,0},{192,64},{1,129},{65,193},{129,1},{193,65... | collective-permute-start | bytes 1572872 | tf_op jit(solution)/shard_map/ppermute | solution.py:324
  10.8 2.2 %collective-permute-start = (f32[128,1024]{1,0:T(8,128)S(1)}, f32[128,1024]{1,0:T(8,128)S(1)}, u32[]{:S(2)}, u32[]{:S(2)}) collective-permute-start(f32[128,1024]{1,0:T(8,128)S(1)} %get-tuple-element.29), channel_id=1, source_target_pairs={{0,64},{64,128},{128,192},{192,0},{1,65},{65,129},{129,193},{193,1... | collective-permute-start | bytes 1572872 | tf_op jit(solution)/shard_map/ppermute | solution.py:324
  13.0 5.5 %collective-permute-done.4.refs_2_ = f32[128,1024]{1,0:T(8,128)S(1)} collective-permute-done((f32[128,1024]{1,0:T(8,128)S(1)}, f32[128,1024]{1,0:T(8,128)S(1)}, u32[]{:S(2)}, u32[]{:S(2)}) %collective-permute-start.4) | collective-permute-done | bytes 524320 | tf_op jit(solution)/shard_map/ppermute | solution.py:324
  18.6 0.8 collective-permute-start.2
  19.3 0.6 column_slices.5.refs_0_
  20.0 0.6 column_slices.4.refs_0_
  20.6 8.8 %collective-permute-done.3.refs_1_ = f32[128,1024]{1,0:T(8,128)S(1)} collective-permute-done((f32[128,1024]{1,0:T(8,128)S(1)}, f32[128,1024]{1,0:T(8,128)S(1)}, u32[]{:S(2)}, u32[]{:S(2)}) %collective-permute-start.3) | collective-permute-done | bytes 524320 | tf_op jit(solution)/shard_map/ppermute | solution.py:324
  29.4 0.5 collective-permute-done.5.refs_3_
  29.9 0.8 copy-done.3
  30.6 1.0 copy-done.4
  31.7 2.7 %gram_lower.2 = (bf16[512,2048]{1,0:T(8,128)(2,1)S(1)}, f32[1280,128]{1,0:T(8,128)S(1)}) custom-call(s32[2]{0:T(128)S(1)} %pad_add_fusion.place_ref, f32[128,1024]{1,0:T(8,128)S(1)} %column_slices.5.refs_0_, f32[128,1024]{1,0:T(8,128)S(1)} %collective-permute-done.3.refs_1_, f32[128,1024]{1,0:T(8,128)S(1)} %collective-permute-done.4.refs_2_, ...), custom_call_target="tpu_custom_call" | custom-call | tf_op jit(solution)/shard_map/gram_lower/pallas_call | solution.py:173
  34.4 6.7 %collective-permute-done.1.refs_2_ = f32[128,1024]{1,0:T(8,128)S(1)} collective-permute-done((f32[128,1024]{1,0:T(8,128)S(1)}, f32[128,1024]{1,0:T(8,128)S(1)}, u32[]{:S(2)}, u32[]{:S(2)}) %collective-permute-start.1) | collective-permute-done | bytes 524320 | tf_op jit(solution)/shard_map/ppermute | solution.py:324
  41.1 7.7 %collective-permute-done.refs_1_ = f32[128,1024]{1,0:T(8,128)S(1)} collective-permute-done((f32[128,1024]{1,0:T(8,128)S(1)}, f32[128,1024]{1,0:T(8,128)S(1)}, u32[]{:S(2)}, u32[]{:S(2)}) %collective-permute-start) | collective-permute-done | bytes 524320 | tf_op jit(solution)/shard_map/ppermute | solution.py:324
  48.7 2.3 %collective-permute-done.2.refs_3_ = f32[128,1024]{1,0:T(8,128)S(1)} collective-permute-done((f32[128,1024]{1,0:T(8,128)S(1)}, f32[128,1024]{1,0:T(8,128)S(1)}, u32[]{:S(2)}, u32[]{:S(2)}) %collective-permute-start.2) | collective-permute-done | bytes 524320 | tf_op jit(solution)/shard_map/ppermute | solution.py:324
  51.1 2.7 %gram_lower.3 = (bf16[512,2048]{1,0:T(8,128)(2,1)S(1)}, f32[640,128]{1,0:T(8,128)S(1)}, f32[640,128]{1,0:T(8,128)S(1)}) custom-call(s32[2]{0:T(128)S(1)} %pad_add_fusion.place_ref, f32[128,1024]{1,0:T(8,128)S(1)} %column_slices.4.refs_0_, f32[128,1024]{1,0:T(8,128)S(1)} %collective-permute-done.refs_1_, f32[128,1024]{1,0:T(8,128)S(1)} %collective-permute-done.1.refs_2_, ...), custom_call_target="tpu_custom_call" | custom-call | tf_op jit(solution)/shard_map/gram_lower/pallas_call | solution.py:173
  53.8 1.3 copy-done.1
  55.2 1.6 %collective-permute-done.6 = f32[640,128]{1,0:T(8,128)S(1)} collective-permute-done((f32[640,128]{1,0:T(8,128)S(1)}, f32[640,128]{1,0:T(8,128)S(1)}, u32[]{:S(2)}, u32[]{:S(2)}) %collective-permute-start.6) | collective-permute-done | bytes 327712 | tf_op jit(solution)/shard_map/ppermute | solution.py:319
  56.8 14.4 %all_to_all.10 = f32[16,40,128]{2,1,0:T(8,128)S(1)} all-to-all(f32[16,40,128]{2,1,0:T(8,128)S(1)} %bitcast.6), channel_id=1, replica_groups=mesh['mode'=4,'y'=4,'z'=8,'core'=2] {'mode','y'}, dimensions={0} | all-to-all | bytes 655360 | tf_op jit(solution)/shard_map/all_to_all | solution.py:344
  71.3 2.0 %collective-permute-start.7 = (f32[40,128]{1,0:T(8,128)S(1)}, f32[40,128]{1,0:T(8,128)S(1)}, u32[]{:S(2)}, u32[]{:S(2)}) collective-permute-start(f32[40,128]{1,0:T(8,128)S(1)} %reduce_sum.9), channel_id=1, source_target_pairs={{0,2},{2,0},{4,6},{6,4},{8,10},{10,8},{12,14},{14,12},{1,3},{3,1},... | collective-permute-start | bytes 61448 | tf_op jit(solution)/shard_map/ppermute | solution.py:334
  73.3 1.9 %collective-permute-done.7 = f32[40,128]{1,0:T(8,128)S(1)} collective-permute-done((f32[40,128]{1,0:T(8,128)S(1)}, f32[40,128]{1,0:T(8,128)S(1)}, u32[]{:S(2)}, u32[]{:S(2)}) %collective-permute-start.7) | collective-permute-done | bytes 20512 | tf_op jit(solution)/shard_map/ppermute | solution.py:334
  75.1 6.3 %collective-permute-start.10 = (f32[40,128]{1,0:T(8,128)S(1)}, f32[40,128]{1,0:T(8,128)S(1)}, u32[]{:S(2)}, u32[]{:S(2)}) collective-permute-start(f32[40,128]{1,0:T(8,128)S(1)} %add.75), channel_id=1, source_target_pairs={{0,12},{2,14},{4,0},{6,2},{8,4},{10,6},{12,8},{14,10},{1,13},{3,15... | collective-permute-start | bytes 61448 | tf_op jit(solution)/shard_map/ppermute | solution.py:324
  81.4 1.1 collective-permute-start.8
  82.5 2.8 %collective-permute-start.9 = (f32[40,128]{1,0:T(8,128)S(1)}, f32[40,128]{1,0:T(8,128)S(1)}, u32[]{:S(2)}, u32[]{:S(2)}) collective-permute-start(f32[40,128]{1,0:T(8,128)S(1)} %add.75), channel_id=1, source_target_pairs={{0,4},{2,6},{4,8},{6,10},{8,12},{10,14},{12,0},{14,2},{1,5},{3,7},... | collective-permute-start | bytes 61448 | tf_op jit(solution)/shard_map/ppermute | solution.py:324
  85.3 3.8 %collective-permute-done.8 = f32[40,128]{1,0:T(8,128)S(1)} collective-permute-done((f32[40,128]{1,0:T(8,128)S(1)}, f32[40,128]{1,0:T(8,128)S(1)}, u32[]{:S(2)}, u32[]{:S(2)}) %collective-permute-start.8) | collective-permute-done | bytes 20512 | tf_op jit(solution)/shard_map/ppermute | solution.py:324
  89.2 12.3 %all_to_all.11 = f32[16,40,128]{2,1,0:T(8,128)S(1)} all-to-all(f32[16,40,128]{2,1,0:T(8,128)S(1)} %broadcast_in_dim.10), channel_id=1, replica_groups=mesh['mode'=4,'y'=4,'z'=8,'core'=2] {'mode','y'}, dimensions={0} | all-to-all | bytes 655360 | tf_op jit(solution)/shard_map/all_to_all | solution.py:330
  101.5 1.6 %collective-permute-done.11.other_ref = f32[640,128]{1,0:T(8,128)S(1)} collective-permute-done((f32[640,128]{1,0:T(8,128)S(1)}, f32[640,128]{1,0:T(8,128)S(1)}, u32[]{:S(2)}, u32[]{:S(2)}) %collective-permute-start.11) | collective-permute-done | bytes 327712 | tf_op jit(solution)/shard_map/ppermute | solution.py:319
  103.1 20.1 %factorize.1 = (f32[1280,128]{1,0:T(8,128)S(1)}, f32[512,128]{1,0:T(8,128)S(1)}) custom-call(s32[2]{0:T(128)S(1)} %pad_add_fusion.place_ref, f32[640,128]{1,0:T(8,128)S(1)} %bitcast.5, f32[640,128]{1,0:T(8,128)S(1)} %collective-permute-done.11.other_ref, f32[512,128]{1,0:T(8,128)S(1)} %copy-done.5), custom_call_target="tpu_custom_call" | custom-call | tf_op jit(solution)/shard_map/factorize/pallas_call | solution.py:279
  123.2 0.2 collective-permute-start.12
  123.4 0.4 collective-permute-start.13
  123.8 2.0 %collective-permute-done.13.other_ref = f32[512,128]{1,0:T(8,128)S(1)} collective-permute-done((f32[512,128]{1,0:T(8,128)S(1)}, f32[512,128]{1,0:T(8,128)S(1)}, u32[]{:S(2)}, u32[]{:S(2)}) %collective-permute-start.13) | collective-permute-done | bytes 262176 | tf_op jit(solution)/shard_map/ppermute | solution.py:319
  125.8 1.3 core_rows.3
  127.1 1.8 %collective-permute-start.14 = (f32[32,1024]{1,0:T(8,128)S(1)}, f32[32,1024]{1,0:T(8,128)S(1)}, u32[]{:S(2)}, u32[]{:S(2)}) collective-permute-start(f32[32,1024]{1,0:T(8,128)S(1)} %get-tuple-element.42), channel_id=1, source_target_pairs={{0,128},{64,192},{128,0},{192,64},{1,129},{65,193},{129,1},{193,65... | collective-permute-start | bytes 393224 | tf_op jit(solution)/shard_map/ppermute | solution.py:324
  128.9 1.7 %collective-permute-start.15 = (f32[32,1024]{1,0:T(8,128)S(1)}, f32[32,1024]{1,0:T(8,128)S(1)}, u32[]{:S(2)}, u32[]{:S(2)}) collective-permute-start(f32[32,1024]{1,0:T(8,128)S(1)} %get-tuple-element.43), channel_id=1, source_target_pairs={{0,64},{64,128},{128,192},{192,0},{1,65},{65,129},{129,193},{193,1... | collective-permute-start | bytes 393224 | tf_op jit(solution)/shard_map/ppermute | solution.py:324
  130.6 0.3 collective-permute-start.16
  130.9 1.6 %copy-done.2 = bf16[512,2048]{1,0:T(8,128)(2,1)S(1)} copy-done((bf16[512,2048]{1,0:T(8,128)(2,1)S(1)}, bf16[512,2048]{1,0:T(8,128)(2,1)}, u32[]{:S(2)}) %copy-start.2) | copy-done | bytes 2097176
  132.5 1.3 core_rows.2
  133.8 1.9 %collective-permute-start.17 = (f32[32,1024]{1,0:T(8,128)S(1)}, f32[32,1024]{1,0:T(8,128)S(1)}, u32[]{:S(2)}, u32[]{:S(2)}) collective-permute-start(f32[32,1024]{1,0:T(8,128)S(1)} %get-tuple-element.46), channel_id=1, source_target_pairs={{0,128},{64,192},{128,0},{192,64},{1,129},{65,193},{129,1},{193,65... | collective-permute-start | bytes 393224 | tf_op jit(solution)/shard_map/ppermute | solution.py:324
  135.7 0.7 broadcast_select_fusion
  136.5 2.1 %collective-permute-start.18 = (f32[32,1024]{1,0:T(8,128)S(1)}, f32[32,1024]{1,0:T(8,128)S(1)}, u32[]{:S(2)}, u32[]{:S(2)}) collective-permute-start(f32[32,1024]{1,0:T(8,128)S(1)} %get-tuple-element.47), channel_id=1, source_target_pairs={{0,64},{64,128},{128,192},{192,0},{1,65},{65,129},{129,193},{193,1... | collective-permute-start | bytes 393224 | tf_op jit(solution)/shard_map/ppermute | solution.py:324
  138.6 2.2 %unpack_triangle.1 = f32[512,512]{1,0:T(8,128)} custom-call(s32[2]{0:T(128)S(1)} %pad_add_fusion.place_ref, f32[1280,128]{1,0:T(8,128)S(1)} %get-tuple-element.34.mine_ref, f32[1280,128]{1,0:T(8,128)} %collective-permute-done.12.other_ref), custom_call_target="tpu_custom_call" | custom-call | tf_op jit(solution)/shard_map/unpack_triangle/pallas_call | solution.py:307
  141.0 2.2 %collective-permute-done.18 = f32[32,1024]{1,0:T(8,128)S(1)} collective-permute-done((f32[32,1024]{1,0:T(8,128)S(1)}, f32[32,1024]{1,0:T(8,128)S(1)}, u32[]{:S(2)}, u32[]{:S(2)}) %collective-permute-start.18) | collective-permute-done | bytes 131104 | tf_op jit(solution)/shard_map/ppermute | solution.py:324
  143.2 3.8 %collective-permute-done.19 = f32[32,1024]{1,0:T(8,128)S(1)} collective-permute-done((f32[32,1024]{1,0:T(8,128)S(1)}, f32[32,1024]{1,0:T(8,128)S(1)}, u32[]{:S(2)}, u32[]{:S(2)}) %collective-permute-start.19) | collective-permute-done | bytes 131104 | tf_op jit(solution)/shard_map/ppermute | solution.py:324
  147.0 1.0 copy-done.6
  (34 shorter events, 0.4 us)
Async XLA Ops:
  2.1 16.4 %collective-permute-start.4 = (f32[128,1024]{1,0:T(8,128)S(1)}, f32[128,1024]{1,0:T(8,128)S(1)}, u32[]{:S(2)}, u32[]{:S(2)}) collective-permute-start(f32[128,1024]{1,0:T(8,128)S(1)} %get-tuple-element.50), channel_id=1, source_target_pairs={{0,128},{64,192},{128,0},{192,64},{1,129},{65,193},{129,1},{193,65... | collective-permute-start | bytes 1572872 | tf_op jit(solution)/shard_map/ppermute | solution.py:324
  3.6 25.8 %collective-permute-start.3 = (f32[128,1024]{1,0:T(8,128)S(1)}, f32[128,1024]{1,0:T(8,128)S(1)}, u32[]{:S(2)}, u32[]{:S(2)}) collective-permute-start(f32[128,1024]{1,0:T(8,128)S(1)} %get-tuple-element.51), channel_id=1, source_target_pairs={{0,64},{64,128},{128,192},{192,0},{1,65},{65,129},{129,193},{193,1... | collective-permute-start | bytes 1572872 | tf_op jit(solution)/shard_map/ppermute | solution.py:324
  5.7 24.2 %collective-permute-start.5 = (f32[128,1024]{1,0:T(8,128)S(1)}, f32[128,1024]{1,0:T(8,128)S(1)}, u32[]{:S(2)}, u32[]{:S(2)}) collective-permute-start(f32[128,1024]{1,0:T(8,128)S(1)} %get-tuple-element.49), channel_id=1, source_target_pairs={{0,192},{64,0},{128,64},{192,128},{1,193},{65,1},{129,65},{193,129... | collective-permute-start | bytes 1572872 | tf_op jit(solution)/shard_map/ppermute | solution.py:324
  5.8 2.2 %copy-start = (f32[128,8192]{1,0:T(8,128)S(1)}, f32[128,8192]{1,0:T(8,128)}, u32[]{:S(2)}) copy-start(f32[128,8192]{1,0:T(8,128)} %source_ref.2) | copy-start | bytes 12582916
  8.7 32.4 %collective-permute-start.1 = (f32[128,1024]{1,0:T(8,128)S(1)}, f32[128,1024]{1,0:T(8,128)S(1)}, u32[]{:S(2)}, u32[]{:S(2)}) collective-permute-start(f32[128,1024]{1,0:T(8,128)S(1)} %get-tuple-element.27), channel_id=1, source_target_pairs={{0,128},{64,192},{128,0},{192,64},{1,129},{65,193},{129,1},{193,65... | collective-permute-start | bytes 1572872 | tf_op jit(solution)/shard_map/ppermute | solution.py:324
  10.8 37.9 %collective-permute-start = (f32[128,1024]{1,0:T(8,128)S(1)}, f32[128,1024]{1,0:T(8,128)S(1)}, u32[]{:S(2)}, u32[]{:S(2)}) collective-permute-start(f32[128,1024]{1,0:T(8,128)S(1)} %get-tuple-element.29), channel_id=1, source_target_pairs={{0,64},{64,128},{128,192},{192,0},{1,65},{65,129},{129,193},{193,1... | collective-permute-start | bytes 1572872 | tf_op jit(solution)/shard_map/ppermute | solution.py:324
  18.6 32.5 %collective-permute-start.2 = (f32[128,1024]{1,0:T(8,128)S(1)}, f32[128,1024]{1,0:T(8,128)S(1)}, u32[]{:S(2)}, u32[]{:S(2)}) collective-permute-start(f32[128,1024]{1,0:T(8,128)S(1)} %get-tuple-element.30), channel_id=1, source_target_pairs={{0,192},{64,0},{128,64},{192,128},{1,193},{65,1},{129,65},{193,129... | collective-permute-start | bytes 1572872 | tf_op jit(solution)/shard_map/ppermute | solution.py:324
  19.9 83.2 %copy-start.5 = (f32[512,128]{1,0:T(8,128)S(1)}, f32[512,128]{1,0:T(8,128)}, u32[]{:S(2)}) copy-start(f32[512,128]{1,0:T(8,128)} %start_ref.1) | copy-start | bytes 786436
  29.9 0.8 copy-start.3
  30.6 1.0 copy-start.4
  53.8 1.3 copy-start.1
  55.2 1.6 %collective-permute-start.6 = (f32[640,128]{1,0:T(8,128)S(1)}, f32[640,128]{1,0:T(8,128)S(1)}, u32[]{:S(2)}, u32[]{:S(2)}) collective-permute-start(f32[640,128]{1,0:T(8,128)S(1)} %get-tuple-element.33), channel_id=1, source_target_pairs={{0,1},{1,0},{2,3},{3,2},{4,5},{5,4},{6,7},{7,6},{8,9},{9,8},{10,11... | collective-permute-start | bytes 983048 | tf_op jit(solution)/shard_map/ppermute | solution.py:319
  71.3 3.9 %collective-permute-start.7 = (f32[40,128]{1,0:T(8,128)S(1)}, f32[40,128]{1,0:T(8,128)S(1)}, u32[]{:S(2)}, u32[]{:S(2)}) collective-permute-start(f32[40,128]{1,0:T(8,128)S(1)} %reduce_sum.9), channel_id=1, source_target_pairs={{0,2},{2,0},{4,6},{6,4},{8,10},{10,8},{12,14},{14,12},{1,3},{3,1},... | collective-permute-start | bytes 61448 | tf_op jit(solution)/shard_map/ppermute | solution.py:334
  75.1 10.2 %collective-permute-start.10 = (f32[40,128]{1,0:T(8,128)S(1)}, f32[40,128]{1,0:T(8,128)S(1)}, u32[]{:S(2)}, u32[]{:S(2)}) collective-permute-start(f32[40,128]{1,0:T(8,128)S(1)} %add.75), channel_id=1, source_target_pairs={{0,12},{2,14},{4,0},{6,2},{8,4},{10,6},{12,8},{14,10},{1,13},{3,15... | collective-permute-start | bytes 61448 | tf_op jit(solution)/shard_map/ppermute | solution.py:324
  81.4 7.7 %collective-permute-start.8 = (f32[40,128]{1,0:T(8,128)S(1)}, f32[40,128]{1,0:T(8,128)S(1)}, u32[]{:S(2)}, u32[]{:S(2)}) collective-permute-start(f32[40,128]{1,0:T(8,128)S(1)} %add.75), channel_id=1, source_target_pairs={{0,8},{2,10},{4,12},{6,14},{8,0},{10,2},{12,4},{14,6},{1,9},{3,11}... | collective-permute-start | bytes 61448 | tf_op jit(solution)/shard_map/ppermute | solution.py:324
  82.5 6.6 %collective-permute-start.9 = (f32[40,128]{1,0:T(8,128)S(1)}, f32[40,128]{1,0:T(8,128)S(1)}, u32[]{:S(2)}, u32[]{:S(2)}) collective-permute-start(f32[40,128]{1,0:T(8,128)S(1)} %add.75), channel_id=1, source_target_pairs={{0,4},{2,6},{4,8},{6,10},{8,12},{10,14},{12,0},{14,2},{1,5},{3,7},... | collective-permute-start | bytes 61448 | tf_op jit(solution)/shard_map/ppermute | solution.py:324
  101.5 1.6 %collective-permute-start.11 = (f32[640,128]{1,0:T(8,128)S(1)}, f32[640,128]{1,0:T(8,128)S(1)}, u32[]{:S(2)}, u32[]{:S(2)}) collective-permute-start(f32[640,128]{1,0:T(8,128)S(1)} %bitcast.4), channel_id=1, source_target_pairs={{0,1},{1,0},{2,3},{3,2},{4,5},{5,4},{6,7},{7,6},{8,9},{9,8},{10,11... | collective-permute-start | bytes 983048 | tf_op jit(solution)/shard_map/ppermute | solution.py:319
  123.2 13.3 %collective-permute-start.12 = (f32[1280,128]{1,0:T(8,128)S(1)}, f32[1280,128]{1,0:T(8,128)}, u32[]{:S(2)}, u32[]{:S(2)}) collective-permute-start(f32[1280,128]{1,0:T(8,128)S(1)} %get-tuple-element.34.mine_ref), channel_id=1, source_target_pairs={{0,1},{1,0},{2,3},{3,2},{4,5},{5,4},{6,7},{7,6},{8,9},{9,8},{10,11... | collective-permute-start | bytes 1966088 | tf_op jit(solution)/shard_map/ppermute | solution.py:319
  123.4 2.4 %collective-permute-start.13 = (f32[512,128]{1,0:T(8,128)S(1)}, f32[512,128]{1,0:T(8,128)S(1)}, u32[]{:S(2)}, u32[]{:S(2)}) collective-permute-start(f32[512,128]{1,0:T(8,128)S(1)} %get-tuple-element.35.mine_ref), channel_id=1, source_target_pairs={{0,1},{1,0},{2,3},{3,2},{4,5},{5,4},{6,7},{7,6},{8,9},{9,8},{10,11... | collective-permute-start | bytes 786440 | tf_op jit(solution)/shard_map/ppermute | solution.py:319
  127.1 13.7 %collective-permute-start.14 = (f32[32,1024]{1,0:T(8,128)S(1)}, f32[32,1024]{1,0:T(8,128)S(1)}, u32[]{:S(2)}, u32[]{:S(2)}) collective-permute-start(f32[32,1024]{1,0:T(8,128)S(1)} %get-tuple-element.42), channel_id=1, source_target_pairs={{0,128},{64,192},{128,0},{192,64},{1,129},{65,193},{129,1},{193,65... | collective-permute-start | bytes 393224 | tf_op jit(solution)/shard_map/ppermute | solution.py:324
  128.9 12.0 %collective-permute-start.15 = (f32[32,1024]{1,0:T(8,128)S(1)}, f32[32,1024]{1,0:T(8,128)S(1)}, u32[]{:S(2)}, u32[]{:S(2)}) collective-permute-start(f32[32,1024]{1,0:T(8,128)S(1)} %get-tuple-element.43), channel_id=1, source_target_pairs={{0,64},{64,128},{128,192},{192,0},{1,65},{65,129},{129,193},{193,1... | collective-permute-start | bytes 393224 | tf_op jit(solution)/shard_map/ppermute | solution.py:324
  130.6 10.3 %collective-permute-start.16 = (f32[32,1024]{1,0:T(8,128)S(1)}, f32[32,1024]{1,0:T(8,128)S(1)}, u32[]{:S(2)}, u32[]{:S(2)}) collective-permute-start(f32[32,1024]{1,0:T(8,128)S(1)} %get-tuple-element.44), channel_id=1, source_target_pairs={{0,192},{64,0},{128,64},{192,128},{1,193},{65,1},{129,65},{193,129... | collective-permute-start | bytes 393224 | tf_op jit(solution)/shard_map/ppermute | solution.py:324
  130.9 1.6 %copy-start.2 = (bf16[512,2048]{1,0:T(8,128)(2,1)S(1)}, bf16[512,2048]{1,0:T(8,128)(2,1)}, u32[]{:S(2)}) copy-start(bf16[512,2048]{1,0:T(8,128)(2,1)} %copy-done.1) | copy-start | bytes 6291460
  133.8 7.2 %collective-permute-start.17 = (f32[32,1024]{1,0:T(8,128)S(1)}, f32[32,1024]{1,0:T(8,128)S(1)}, u32[]{:S(2)}, u32[]{:S(2)}) collective-permute-start(f32[32,1024]{1,0:T(8,128)S(1)} %get-tuple-element.46), channel_id=1, source_target_pairs={{0,128},{64,192},{128,0},{192,64},{1,129},{65,193},{129,1},{193,65... | collective-permute-start | bytes 393224 | tf_op jit(solution)/shard_map/ppermute | solution.py:324
  136.5 6.7 %collective-permute-start.18 = (f32[32,1024]{1,0:T(8,128)S(1)}, f32[32,1024]{1,0:T(8,128)S(1)}, u32[]{:S(2)}, u32[]{:S(2)}) collective-permute-start(f32[32,1024]{1,0:T(8,128)S(1)} %get-tuple-element.47), channel_id=1, source_target_pairs={{0,64},{64,128},{128,192},{192,0},{1,65},{65,129},{129,193},{193,1... | collective-permute-start | bytes 393224 | tf_op jit(solution)/shard_map/ppermute | solution.py:324
  140.8 6.2 %collective-permute-start.19 = (f32[32,1024]{1,0:T(8,128)S(1)}, f32[32,1024]{1,0:T(8,128)S(1)}, u32[]{:S(2)}, u32[]{:S(2)}) collective-permute-start(f32[32,1024]{1,0:T(8,128)S(1)} %get-tuple-element.48), channel_id=1, source_target_pairs={{0,192},{64,0},{128,64},{192,128},{1,193},{65,1},{129,65},{193,129... | collective-permute-start | bytes 393224 | tf_op jit(solution)/shard_map/ppermute | solution.py:324
  147.0 1.0 copy-start.6

commit v4 on v3

--- a/solution.py
+++ b/solution.py
@@ -40,17 +40,18 @@
         top = rows[t]
         unit = jnp.where(lane == first + sub, 1.0, 0.0)
         recips = []
-        mults = {i: [] for i in range(t + 1, n // 8)}
+        left = {i: jnp.where(inside, 0.0, rows[i]) for i in range(t + 1, n // 8)}
         for j in range(8):
             recip = 1.0 / spread(own[j][j : j + 1, :])
             recips.append(recip)
+            source = spread(jnp.where(inside, unit, top)[j : j + 1, :])
             mult = jnp.where(sub > j, own[j] * recip, 0.0)
             top = top - mult * spread(top[j : j + 1, :])
             unit = unit - mult * spread(unit[j : j + 1, :])
             pivot_row = {l: spread(own[l][j : j + 1, :]) for l in range(j + 1, 8)}
             for i in range(t + 1, n // 8):
                 mult = cols[i][j] * recip
-                mults[i].append(mult)
+                left[i] = left[i] - mult * source
                 for l in range(j + 1, 8):
                     cols[i][l] = cols[i][l] - mult * pivot_row[l]
             for l in range(j + 1, 8):
@@ -62,12 +63,7 @@
         inverse_ref[first : first + 8, :] = scale * jnp.where(lane < first, top, unit)
         if upper_ref is not None:
             upper_ref[first : first + 8, :] = jnp.where(lane >= first + sub, scale * top, 0.0)
-        source = jnp.where(inside, unit, top)
-        for i in range(t + 1, n // 8):
-            left = jnp.where(inside, 0.0, rows[i])
-            for j in range(8):
-                left = left - mults[i][j] * spread(source[j : j + 1, :])
-            rows[i] = left
+        rows[t + 1 :] = [left[i] for i in range(t + 1, n // 8)]
 
 
 def block_index(i, j):

time: 148 us -> 148 us (level)
  no operation moved by 1% of the time
where the time goes in v4:
time: 148 us; the launch traced here: 147 us
  waiting for transfers between devices  48.4 us (33%)
  Pallas kernels  31.1 us (21%)
  starting transfers between devices  29.6 us (20%)
  blocking collectives  26.7 us (18%)
  local copies, waits for them, and re-layouts  9.61 us (6%)
    ppermute x15, waiting for transfers between devices, shift(): return lax.ppermute(value, axis, [(i, (i + by) % n) for i in range(n)])  41.3 us
    ppermute x15, starting transfers between devices, shift(): return lax.ppermute(value, axis, [(i, (i + by) % n) for i in range(n)])  26.8 us
    pallas_call x1, Pallas kernels, factorize(): pl.pallas_call(functools.partial(factor_kernel, scale), in_specs=[SMEM, V...  19.1 us
    all_to_all x1, blocking collectives, sum_everywhere(): lax.all_to_all(mine.reshape(n, rows // n, lanes), plane, 0, 0, tiled=True)  14.4 us
    all_to_all x1, blocking collectives, spread_out(): return lax.all_to_all(copies, axes, 0, 0, tiled=True)  12.3 us
    unnamed x14, local copies, waits for them, and re-layouts  7.92 us
    pallas_call x2, Pallas kernels, gram_lower(): pl.pallas_call(functools.partial(gram_kernel, prior is not None, final),...  5.39 us
    ppermute x4, waiting for transfers between devices, swap_cores(): return lax.ppermute(value, 'core', [(0, 1), (1, 0)])  5.22 us
  transfers between devices with their start and end apart: 20, of which 13 were waited for; matrix products, arithmetic and copies ran while one was open for 1% of the time, Pallas kernels for 6%

profile of v4, /device:TPU:6, one launch (start us, length us, event | category | flops | bytes accessed | tf_op | source)
XLA Modules:
  0.0 147.2 jit_solution(4548313048552003360)
XLA Ops:
  0.6 1.5 constant_dynamic-slice_fusion
  2.1 1.5 %collective-permute-start.4 = (f32[128,1024]{1,0:T(8,128)S(1)}, f32[128,1024]{1,0:T(8,128)S(1)}, u32[]{:S(2)}, u32[]{:S(2)}) collective-permute-start(f32[128,1024]{1,0:T(8,128)S(1)} %get-tuple-element.50), channel_id=1, source_target_pairs={{0,128},{64,192},{128,0},{192,64},{1,129},{65,193},{129,1},{193,65... | collective-permute-start | bytes 1572872 | tf_op jit(solution)/shard_map/ppermute | solution.py:320
  3.6 2.1 %collective-permute-start.3 = (f32[128,1024]{1,0:T(8,128)S(1)}, f32[128,1024]{1,0:T(8,128)S(1)}, u32[]{:S(2)}, u32[]{:S(2)}) collective-permute-start(f32[128,1024]{1,0:T(8,128)S(1)} %get-tuple-element.51), channel_id=1, source_target_pairs={{0,64},{64,128},{128,192},{192,0},{1,65},{65,129},{129,193},{193,1... | collective-permute-start | bytes 1572872 | tf_op jit(solution)/shard_map/ppermute | solution.py:320
  5.8 2.2 %copy-done = f32[128,8192]{1,0:T(8,128)S(1)} copy-done((f32[128,8192]{1,0:T(8,128)S(1)}, f32[128,8192]{1,0:T(8,128)}, u32[]{:S(2)}) %copy-start) | copy-done | bytes 4194328
  8.0 0.7 column_slices.3
  8.7 2.1 %collective-permute-start.1 = (f32[128,1024]{1,0:T(8,128)S(1)}, f32[128,1024]{1,0:T(8,128)S(1)}, u32[]{:S(2)}, u32[]{:S(2)}) collective-permute-start(f32[128,1024]{1,0:T(8,128)S(1)} %get-tuple-element.27), channel_id=1, source_target_pairs={{0,128},{64,192},{128,0},{192,64},{1,129},{65,193},{129,1},{193,65... | collective-permute-start | bytes 1572872 | tf_op jit(solution)/shard_map/ppermute | solution.py:320
  10.8 2.2 %collective-permute-start = (f32[128,1024]{1,0:T(8,128)S(1)}, f32[128,1024]{1,0:T(8,128)S(1)}, u32[]{:S(2)}, u32[]{:S(2)}) collective-permute-start(f32[128,1024]{1,0:T(8,128)S(1)} %get-tuple-element.29), channel_id=1, source_target_pairs={{0,64},{64,128},{128,192},{192,0},{1,65},{65,129},{129,193},{193,1... | collective-permute-start | bytes 1572872 | tf_op jit(solution)/shard_map/ppermute | solution.py:320
  13.0 5.5 %collective-permute-done.4.refs_2_ = f32[128,1024]{1,0:T(8,128)S(1)} collective-permute-done((f32[128,1024]{1,0:T(8,128)S(1)}, f32[128,1024]{1,0:T(8,128)S(1)}, u32[]{:S(2)}, u32[]{:S(2)}) %collective-permute-start.4) | collective-permute-done | bytes 524320 | tf_op jit(solution)/shard_map/ppermute | solution.py:320
  18.6 0.8 collective-permute-start.2
  19.3 0.6 column_slices.5.refs_0_
  20.0 0.6 column_slices.4.refs_0_
  20.6 8.8 %collective-permute-done.3.refs_1_ = f32[128,1024]{1,0:T(8,128)S(1)} collective-permute-done((f32[128,1024]{1,0:T(8,128)S(1)}, f32[128,1024]{1,0:T(8,128)S(1)}, u32[]{:S(2)}, u32[]{:S(2)}) %collective-permute-start.3) | collective-permute-done | bytes 524320 | tf_op jit(solution)/shard_map/ppermute | solution.py:320
  29.4 0.5 collective-permute-done.5.refs_3_
  29.9 0.8 copy-done.3
  30.6 1.0 copy-done.4
  31.7 2.7 %gram_lower.2 = (bf16[512,2048]{1,0:T(8,128)(2,1)S(1)}, f32[1280,128]{1,0:T(8,128)S(1)}) custom-call(s32[2]{0:T(128)S(1)} %pad_add_fusion.place_ref, f32[128,1024]{1,0:T(8,128)S(1)} %column_slices.5.refs_0_, f32[128,1024]{1,0:T(8,128)S(1)} %collective-permute-done.3.refs_1_, f32[128,1024]{1,0:T(8,128)S(1)} %collective-permute-done.4.refs_2_, ...), custom_call_target="tpu_custom_call" | custom-call | tf_op jit(solution)/shard_map/gram_lower/pallas_call | solution.py:169
  34.4 6.7 %collective-permute-done.1.refs_2_ = f32[128,1024]{1,0:T(8,128)S(1)} collective-permute-done((f32[128,1024]{1,0:T(8,128)S(1)}, f32[128,1024]{1,0:T(8,128)S(1)}, u32[]{:S(2)}, u32[]{:S(2)}) %collective-permute-start.1) | collective-permute-done | bytes 524320 | tf_op jit(solution)/shard_map/ppermute | solution.py:320
  41.1 7.7 %collective-permute-done.refs_1_ = f32[128,1024]{1,0:T(8,128)S(1)} collective-permute-done((f32[128,1024]{1,0:T(8,128)S(1)}, f32[128,1024]{1,0:T(8,128)S(1)}, u32[]{:S(2)}, u32[]{:S(2)}) %collective-permute-start) | collective-permute-done | bytes 524320 | tf_op jit(solution)/shard_map/ppermute | solution.py:320
  48.7 2.3 %collective-permute-done.2.refs_3_ = f32[128,1024]{1,0:T(8,128)S(1)} collective-permute-done((f32[128,1024]{1,0:T(8,128)S(1)}, f32[128,1024]{1,0:T(8,128)S(1)}, u32[]{:S(2)}, u32[]{:S(2)}) %collective-permute-start.2) | collective-permute-done | bytes 524320 | tf_op jit(solution)/shard_map/ppermute | solution.py:320
  51.1 2.7 %gram_lower.3 = (bf16[512,2048]{1,0:T(8,128)(2,1)S(1)}, f32[640,128]{1,0:T(8,128)S(1)}, f32[640,128]{1,0:T(8,128)S(1)}) custom-call(s32[2]{0:T(128)S(1)} %pad_add_fusion.place_ref, f32[128,1024]{1,0:T(8,128)S(1)} %column_slices.4.refs_0_, f32[128,1024]{1,0:T(8,128)S(1)} %collective-permute-done.refs_1_, f32[128,1024]{1,0:T(8,128)S(1)} %collective-permute-done.1.refs_2_, ...), custom_call_target="tpu_custom_call" | custom-call | tf_op jit(solution)/shard_map/gram_lower/pallas_call | solution.py:169
  53.8 1.3 copy-done.1
  55.2 1.6 %collective-permute-done.6 = f32[640,128]{1,0:T(8,128)S(1)} collective-permute-done((f32[640,128]{1,0:T(8,128)S(1)}, f32[640,128]{1,0:T(8,128)S(1)}, u32[]{:S(2)}, u32[]{:S(2)}) %collective-permute-start.6) | collective-permute-done | bytes 327712 | tf_op jit(solution)/shard_map/ppermute | solution.py:315
  56.8 14.4 %all_to_all.10 = f32[16,40,128]{2,1,0:T(8,128)S(1)} all-to-all(f32[16,40,128]{2,1,0:T(8,128)S(1)} %bitcast.6), channel_id=1, replica_groups=mesh['mode'=4,'y'=4,'z'=8,'core'=2] {'mode','y'}, dimensions={0} | all-to-all | bytes 655360 | tf_op jit(solution)/shard_map/all_to_all | solution.py:340
  71.3 2.0 %collective-permute-start.7 = (f32[40,128]{1,0:T(8,128)S(1)}, f32[40,128]{1,0:T(8,128)S(1)}, u32[]{:S(2)}, u32[]{:S(2)}) collective-permute-start(f32[40,128]{1,0:T(8,128)S(1)} %reduce_sum.9), channel_id=1, source_target_pairs={{0,2},{2,0},{4,6},{6,4},{8,10},{10,8},{12,14},{14,12},{1,3},{3,1},... | collective-permute-start | bytes 61448 | tf_op jit(solution)/shard_map/ppermute | solution.py:330
  73.3 1.9 %collective-permute-done.7 = f32[40,128]{1,0:T(8,128)S(1)} collective-permute-done((f32[40,128]{1,0:T(8,128)S(1)}, f32[40,128]{1,0:T(8,128)S(1)}, u32[]{:S(2)}, u32[]{:S(2)}) %collective-permute-start.7) | collective-permute-done | bytes 20512 | tf_op jit(solution)/shard_map/ppermute | solution.py:330
  75.1 6.3 %collective-permute-start.10 = (f32[40,128]{1,0:T(8,128)S(1)}, f32[40,128]{1,0:T(8,128)S(1)}, u32[]{:S(2)}, u32[]{:S(2)}) collective-permute-start(f32[40,128]{1,0:T(8,128)S(1)} %add.75), channel_id=1, source_target_pairs={{0,12},{2,14},{4,0},{6,2},{8,4},{10,6},{12,8},{14,10},{1,13},{3,15... | collective-permute-start | bytes 61448 | tf_op jit(solution)/shard_map/ppermute | solution.py:320
  81.4 1.1 collective-permute-start.8
  82.5 2.8 %collective-permute-start.9 = (f32[40,128]{1,0:T(8,128)S(1)}, f32[40,128]{1,0:T(8,128)S(1)}, u32[]{:S(2)}, u32[]{:S(2)}) collective-permute-start(f32[40,128]{1,0:T(8,128)S(1)} %add.75), channel_id=1, source_target_pairs={{0,4},{2,6},{4,8},{6,10},{8,12},{10,14},{12,0},{14,2},{1,5},{3,7},... | collective-permute-start | bytes 61448 | tf_op jit(solution)/shard_map/ppermute | solution.py:320
  85.3 3.8 %collective-permute-done.8 = f32[40,128]{1,0:T(8,128)S(1)} collective-permute-done((f32[40,128]{1,0:T(8,128)S(1)}, f32[40,128]{1,0:T(8,128)S(1)}, u32[]{:S(2)}, u32[]{:S(2)}) %collective-permute-start.8) | collective-permute-done | bytes 20512 | tf_op jit(solution)/shard_map/ppermute | solution.py:320
  89.2 12.3 %all_to_all.11 = f32[16,40,128]{2,1,0:T(8,128)S(1)} all-to-all(f32[16,40,128]{2,1,0:T(8,128)S(1)} %broadcast_in_dim.10), channel_id=1, replica_groups=mesh['mode'=4,'y'=4,'z'=8,'core'=2] {'mode','y'}, dimensions={0} | all-to-all | bytes 655360 | tf_op jit(solution)/shard_map/all_to_all | solution.py:326
  101.5 1.6 %collective-permute-done.11.other_ref = f32[640,128]{1,0:T(8,128)S(1)} collective-permute-done((f32[640,128]{1,0:T(8,128)S(1)}, f32[640,128]{1,0:T(8,128)S(1)}, u32[]{:S(2)}, u32[]{:S(2)}) %collective-permute-start.11) | collective-permute-done | bytes 327712 | tf_op jit(solution)/shard_map/ppermute | solution.py:315
  103.1 19.1 %factorize.1 = (f32[1280,128]{1,0:T(8,128)S(1)}, f32[512,128]{1,0:T(8,128)S(1)}) custom-call(s32[2]{0:T(128)S(1)} %pad_add_fusion.place_ref, f32[640,128]{1,0:T(8,128)S(1)} %bitcast.5, f32[640,128]{1,0:T(8,128)S(1)} %collective-permute-done.11.other_ref, f32[512,128]{1,0:T(8,128)S(1)} %copy-done.5), custom_call_target="tpu_custom_call" | custom-call | tf_op jit(solution)/shard_map/factorize/pallas_call | solution.py:275
  122.2 0.7 collective-permute-start.12
  122.9 0.1 collective-permute-start.13
  123.0 2.0 %collective-permute-done.13.other_ref = f32[512,128]{1,0:T(8,128)S(1)} collective-permute-done((f32[512,128]{1,0:T(8,128)S(1)}, f32[512,128]{1,0:T(8,128)S(1)}, u32[]{:S(2)}, u32[]{:S(2)}) %collective-permute-start.13) | collective-permute-done | bytes 262176 | tf_op jit(solution)/shard_map/ppermute | solution.py:315
  125.0 1.3 core_rows.3
  126.3 1.8 %collective-permute-start.14 = (f32[32,1024]{1,0:T(8,128)S(1)}, f32[32,1024]{1,0:T(8,128)S(1)}, u32[]{:S(2)}, u32[]{:S(2)}) collective-permute-start(f32[32,1024]{1,0:T(8,128)S(1)} %get-tuple-element.42), channel_id=1, source_target_pairs={{0,128},{64,192},{128,0},{192,64},{1,129},{65,193},{129,1},{193,65... | collective-permute-start | bytes 393224 | tf_op jit(solution)/shard_map/ppermute | solution.py:320
  128.1 1.7 %collective-permute-start.15 = (f32[32,1024]{1,0:T(8,128)S(1)}, f32[32,1024]{1,0:T(8,128)S(1)}, u32[]{:S(2)}, u32[]{:S(2)}) collective-permute-start(f32[32,1024]{1,0:T(8,128)S(1)} %get-tuple-element.43), channel_id=1, source_target_pairs={{0,64},{64,128},{128,192},{192,0},{1,65},{65,129},{129,193},{193,1... | collective-permute-start | bytes 393224 | tf_op jit(solution)/shard_map/ppermute | solution.py:320
  129.8 0.3 collective-permute-start.16
  130.1 1.6 %copy-done.2 = bf16[512,2048]{1,0:T(8,128)(2,1)S(1)} copy-done((bf16[512,2048]{1,0:T(8,128)(2,1)S(1)}, bf16[512,2048]{1,0:T(8,128)(2,1)}, u32[]{:S(2)}) %copy-start.2) | copy-done | bytes 2097176
  131.7 1.3 core_rows.2
  133.0 1.9 %collective-permute-start.17 = (f32[32,1024]{1,0:T(8,128)S(1)}, f32[32,1024]{1,0:T(8,128)S(1)}, u32[]{:S(2)}, u32[]{:S(2)}) collective-permute-start(f32[32,1024]{1,0:T(8,128)S(1)} %get-tuple-element.46), channel_id=1, source_target_pairs={{0,128},{64,192},{128,0},{192,64},{1,129},{65,193},{129,1},{193,65... | collective-permute-start | bytes 393224 | tf_op jit(solution)/shard_map/ppermute | solution.py:320
  134.9 0.7 broadcast_select_fusion
  135.7 2.1 %collective-permute-start.18 = (f32[32,1024]{1,0:T(8,128)S(1)}, f32[32,1024]{1,0:T(8,128)S(1)}, u32[]{:S(2)}, u32[]{:S(2)}) collective-permute-start(f32[32,1024]{1,0:T(8,128)S(1)} %get-tuple-element.47), channel_id=1, source_target_pairs={{0,64},{64,128},{128,192},{192,0},{1,65},{65,129},{129,193},{193,1... | collective-permute-start | bytes 393224 | tf_op jit(solution)/shard_map/ppermute | solution.py:320
  137.8 2.2 %unpack_triangle.1 = f32[512,512]{1,0:T(8,128)} custom-call(s32[2]{0:T(128)S(1)} %pad_add_fusion.place_ref, f32[1280,128]{1,0:T(8,128)S(1)} %get-tuple-element.34.mine_ref, f32[1280,128]{1,0:T(8,128)} %collective-permute-done.12.other_ref), custom_call_target="tpu_custom_call" | custom-call | tf_op jit(solution)/shard_map/unpack_triangle/pallas_call | solution.py:303
  140.2 2.4 %collective-permute-done.18 = f32[32,1024]{1,0:T(8,128)S(1)} collective-permute-done((f32[32,1024]{1,0:T(8,128)S(1)}, f32[32,1024]{1,0:T(8,128)S(1)}, u32[]{:S(2)}, u32[]{:S(2)}) %collective-permute-start.18) | collective-permute-done | bytes 131104 | tf_op jit(solution)/shard_map/ppermute | solution.py:320
  142.6 3.5 %collective-permute-done.19 = f32[32,1024]{1,0:T(8,128)S(1)} collective-permute-done((f32[32,1024]{1,0:T(8,128)S(1)}, f32[32,1024]{1,0:T(8,128)S(1)}, u32[]{:S(2)}, u32[]{:S(2)}) %collective-permute-start.19) | collective-permute-done | bytes 131104 | tf_op jit(solution)/shard_map/ppermute | solution.py:320
  146.2 1.0 copy-done.6
  (34 shorter events, 0.4 us)
Async XLA Ops:
  2.1 16.4 %collective-permute-start.4 = (f32[128,1024]{1,0:T(8,128)S(1)}, f32[128,1024]{1,0:T(8,128)S(1)}, u32[]{:S(2)}, u32[]{:S(2)}) collective-permute-start(f32[128,1024]{1,0:T(8,128)S(1)} %get-tuple-element.50), channel_id=1, source_target_pairs={{0,128},{64,192},{128,0},{192,64},{1,129},{65,193},{129,1},{193,65... | collective-permute-start | bytes 1572872 | tf_op jit(solution)/shard_map/ppermute | solution.py:320
  3.6 25.8 %collective-permute-start.3 = (f32[128,1024]{1,0:T(8,128)S(1)}, f32[128,1024]{1,0:T(8,128)S(1)}, u32[]{:S(2)}, u32[]{:S(2)}) collective-permute-start(f32[128,1024]{1,0:T(8,128)S(1)} %get-tuple-element.51), channel_id=1, source_target_pairs={{0,64},{64,128},{128,192},{192,0},{1,65},{65,129},{129,193},{193,1... | collective-permute-start | bytes 1572872 | tf_op jit(solution)/shard_map/ppermute | solution.py:320
  5.7 24.2 %collective-permute-start.5 = (f32[128,1024]{1,0:T(8,128)S(1)}, f32[128,1024]{1,0:T(8,128)S(1)}, u32[]{:S(2)}, u32[]{:S(2)}) collective-permute-start(f32[128,1024]{1,0:T(8,128)S(1)} %get-tuple-element.49), channel_id=1, source_target_pairs={{0,192},{64,0},{128,64},{192,128},{1,193},{65,1},{129,65},{193,129... | collective-permute-start | bytes 1572872 | tf_op jit(solution)/shard_map/ppermute | solution.py:320
  5.8 2.2 %copy-start = (f32[128,8192]{1,0:T(8,128)S(1)}, f32[128,8192]{1,0:T(8,128)}, u32[]{:S(2)}) copy-start(f32[128,8192]{1,0:T(8,128)} %source_ref.2) | copy-start | bytes 12582916
  8.7 32.4 %collective-permute-start.1 = (f32[128,1024]{1,0:T(8,128)S(1)}, f32[128,1024]{1,0:T(8,128)S(1)}, u32[]{:S(2)}, u32[]{:S(2)}) collective-permute-start(f32[128,1024]{1,0:T(8,128)S(1)} %get-tuple-element.27), channel_id=1, source_target_pairs={{0,128},{64,192},{128,0},{192,64},{1,129},{65,193},{129,1},{193,65... | collective-permute-start | bytes 1572872 | tf_op jit(solution)/shard_map/ppermute | solution.py:320
  10.8 37.9 %collective-permute-start = (f32[128,1024]{1,0:T(8,128)S(1)}, f32[128,1024]{1,0:T(8,128)S(1)}, u32[]{:S(2)}, u32[]{:S(2)}) collective-permute-start(f32[128,1024]{1,0:T(8,128)S(1)} %get-tuple-element.29), channel_id=1, source_target_pairs={{0,64},{64,128},{128,192},{192,0},{1,65},{65,129},{129,193},{193,1... | collective-permute-start | bytes 1572872 | tf_op jit(solution)/shard_map/ppermute | solution.py:320
  18.6 32.5 %collective-permute-start.2 = (f32[128,1024]{1,0:T(8,128)S(1)}, f32[128,1024]{1,0:T(8,128)S(1)}, u32[]{:S(2)}, u32[]{:S(2)}) collective-permute-start(f32[128,1024]{1,0:T(8,128)S(1)} %get-tuple-element.30), channel_id=1, source_target_pairs={{0,192},{64,0},{128,64},{192,128},{1,193},{65,1},{129,65},{193,129... | collective-permute-start | bytes 1572872 | tf_op jit(solution)/shard_map/ppermute | solution.py:320
  19.9 83.2 %copy-start.5 = (f32[512,128]{1,0:T(8,128)S(1)}, f32[512,128]{1,0:T(8,128)}, u32[]{:S(2)}) copy-start(f32[512,128]{1,0:T(8,128)} %start_ref.1) | copy-start | bytes 786436
  29.9 0.8 copy-start.3
  30.6 1.0 copy-start.4
  53.8 1.3 copy-start.1
  55.2 1.6 %collective-permute-start.6 = (f32[640,128]{1,0:T(8,128)S(1)}, f32[640,128]{1,0:T(8,128)S(1)}, u32[]{:S(2)}, u32[]{:S(2)}) collective-permute-start(f32[640,128]{1,0:T(8,128)S(1)} %get-tuple-element.33), channel_id=1, source_target_pairs={{0,1},{1,0},{2,3},{3,2},{4,5},{5,4},{6,7},{7,6},{8,9},{9,8},{10,11... | collective-permute-start | bytes 983048 | tf_op jit(solution)/shard_map/ppermute | solution.py:315
  71.3 3.9 %collective-permute-start.7 = (f32[40,128]{1,0:T(8,128)S(1)}, f32[40,128]{1,0:T(8,128)S(1)}, u32[]{:S(2)}, u32[]{:S(2)}) collective-permute-start(f32[40,128]{1,0:T(8,128)S(1)} %reduce_sum.9), channel_id=1, source_target_pairs={{0,2},{2,0},{4,6},{6,4},{8,10},{10,8},{12,14},{14,12},{1,3},{3,1},... | collective-permute-start | bytes 61448 | tf_op jit(solution)/shard_map/ppermute | solution.py:330
  75.1 10.2 %collective-permute-start.10 = (f32[40,128]{1,0:T(8,128)S(1)}, f32[40,128]{1,0:T(8,128)S(1)}, u32[]{:S(2)}, u32[]{:S(2)}) collective-permute-start(f32[40,128]{1,0:T(8,128)S(1)} %add.75), channel_id=1, source_target_pairs={{0,12},{2,14},{4,0},{6,2},{8,4},{10,6},{12,8},{14,10},{1,13},{3,15... | collective-permute-start | bytes 61448 | tf_op jit(solution)/shard_map/ppermute | solution.py:320
  81.4 7.7 %collective-permute-start.8 = (f32[40,128]{1,0:T(8,128)S(1)}, f32[40,128]{1,0:T(8,128)S(1)}, u32[]{:S(2)}, u32[]{:S(2)}) collective-permute-start(f32[40,128]{1,0:T(8,128)S(1)} %add.75), channel_id=1, source_target_pairs={{0,8},{2,10},{4,12},{6,14},{8,0},{10,2},{12,4},{14,6},{1,9},{3,11}... | collective-permute-start | bytes 61448 | tf_op jit(solution)/shard_map/ppermute | solution.py:320
  82.5 6.6 %collective-permute-start.9 = (f32[40,128]{1,0:T(8,128)S(1)}, f32[40,128]{1,0:T(8,128)S(1)}, u32[]{:S(2)}, u32[]{:S(2)}) collective-permute-start(f32[40,128]{1,0:T(8,128)S(1)} %add.75), channel_id=1, source_target_pairs={{0,4},{2,6},{4,8},{6,10},{8,12},{10,14},{12,0},{14,2},{1,5},{3,7},... | collective-permute-start | bytes 61448 | tf_op jit(solution)/shard_map/ppermute | solution.py:320
  101.5 1.6 %collective-permute-start.11 = (f32[640,128]{1,0:T(8,128)S(1)}, f32[640,128]{1,0:T(8,128)S(1)}, u32[]{:S(2)}, u32[]{:S(2)}) collective-permute-start(f32[640,128]{1,0:T(8,128)S(1)} %bitcast.4), channel_id=1, source_target_pairs={{0,1},{1,0},{2,3},{3,2},{4,5},{5,4},{6,7},{7,6},{8,9},{9,8},{10,11... | collective-permute-start | bytes 983048 | tf_op jit(solution)/shard_map/ppermute | solution.py:315
  122.2 13.5 %collective-permute-start.12 = (f32[1280,128]{1,0:T(8,128)S(1)}, f32[1280,128]{1,0:T(8,128)}, u32[]{:S(2)}, u32[]{:S(2)}) collective-permute-start(f32[1280,128]{1,0:T(8,128)S(1)} %get-tuple-element.34.mine_ref), channel_id=1, source_target_pairs={{0,1},{1,0},{2,3},{3,2},{4,5},{5,4},{6,7},{7,6},{8,9},{9,8},{10,11... | collective-permute-start | bytes 1966088 | tf_op jit(solution)/shard_map/ppermute | solution.py:315
  122.9 2.1 %collective-permute-start.13 = (f32[512,128]{1,0:T(8,128)S(1)}, f32[512,128]{1,0:T(8,128)S(1)}, u32[]{:S(2)}, u32[]{:S(2)}) collective-permute-start(f32[512,128]{1,0:T(8,128)S(1)} %get-tuple-element.35.mine_ref), channel_id=1, source_target_pairs={{0,1},{1,0},{2,3},{3,2},{4,5},{5,4},{6,7},{7,6},{8,9},{9,8},{10,11... | collective-permute-start | bytes 786440 | tf_op jit(solution)/shard_map/ppermute | solution.py:315
  126.3 13.7 %collective-permute-start.14 = (f32[32,1024]{1,0:T(8,128)S(1)}, f32[32,1024]{1,0:T(8,128)S(1)}, u32[]{:S(2)}, u32[]{:S(2)}) collective-permute-start(f32[32,1024]{1,0:T(8,128)S(1)} %get-tuple-element.42), channel_id=1, source_target_pairs={{0,128},{64,192},{128,0},{192,64},{1,129},{65,193},{129,1},{193,65... | collective-permute-start | bytes 393224 | tf_op jit(solution)/shard_map/ppermute | solution.py:320
  128.1 12.0 %collective-permute-start.15 = (f32[32,1024]{1,0:T(8,128)S(1)}, f32[32,1024]{1,0:T(8,128)S(1)}, u32[]{:S(2)}, u32[]{:S(2)}) collective-permute-start(f32[32,1024]{1,0:T(8,128)S(1)} %get-tuple-element.43), channel_id=1, source_target_pairs={{0,64},{64,128},{128,192},{192,0},{1,65},{65,129},{129,193},{193,1... | collective-permute-start | bytes 393224 | tf_op jit(solution)/shard_map/ppermute | solution.py:320
  129.8 10.3 %collective-permute-start.16 = (f32[32,1024]{1,0:T(8,128)S(1)}, f32[32,1024]{1,0:T(8,128)S(1)}, u32[]{:S(2)}, u32[]{:S(2)}) collective-permute-start(f32[32,1024]{1,0:T(8,128)S(1)} %get-tuple-element.44), channel_id=1, source_target_pairs={{0,192},{64,0},{128,64},{192,128},{1,193},{65,1},{129,65},{193,129... | collective-permute-start | bytes 393224 | tf_op jit(solution)/shard_map/ppermute | solution.py:320
  130.1 1.6 %copy-start.2 = (bf16[512,2048]{1,0:T(8,128)(2,1)S(1)}, bf16[512,2048]{1,0:T(8,128)(2,1)}, u32[]{:S(2)}) copy-start(bf16[512,2048]{1,0:T(8,128)(2,1)} %copy-done.1) | copy-start | bytes 6291460
  133.0 7.2 %collective-permute-start.17 = (f32[32,1024]{1,0:T(8,128)S(1)}, f32[32,1024]{1,0:T(8,128)S(1)}, u32[]{:S(2)}, u32[]{:S(2)}) collective-permute-start(f32[32,1024]{1,0:T(8,128)S(1)} %get-tuple-element.46), channel_id=1, source_target_pairs={{0,128},{64,192},{128,0},{192,64},{1,129},{65,193},{129,1},{193,65... | collective-permute-start | bytes 393224 | tf_op jit(solution)/shard_map/ppermute | solution.py:320
  135.7 6.9 %collective-permute-start.18 = (f32[32,1024]{1,0:T(8,128)S(1)}, f32[32,1024]{1,0:T(8,128)S(1)}, u32[]{:S(2)}, u32[]{:S(2)}) collective-permute-start(f32[32,1024]{1,0:T(8,128)S(1)} %get-tuple-element.47), channel_id=1, source_target_pairs={{0,64},{64,128},{128,192},{192,0},{1,65},{65,129},{129,193},{193,1... | collective-permute-start | bytes 393224 | tf_op jit(solution)/shard_map/ppermute | solution.py:320
  140.0 6.2 %collective-permute-start.19 = (f32[32,1024]{1,0:T(8,128)S(1)}, f32[32,1024]{1,0:T(8,128)S(1)}, u32[]{:S(2)}, u32[]{:S(2)}) collective-permute-start(f32[32,1024]{1,0:T(8,128)S(1)} %get-tuple-element.48), channel_id=1, source_target_pairs={{0,192},{64,0},{128,64},{192,128},{1,193},{65,1},{129,65},{193,129... | collective-permute-start | bytes 393224 | tf_op jit(solution)/shard_map/ppermute | solution.py:320
  146.2 1.0 copy-start.6

commit v5 on v4

--- a/solution.py
+++ b/solution.py
@@ -230,17 +230,17 @@
         def panel(p, carry):
             here = pl.ds(pl.multiple_of(p * NB, NB), NB)
             cholesky_block(full_ref[here, here], inv_ref, up_ref)
-            column = dot_exact(full_ref[:, here], inv_ref[...], NT)
+            column = dot_exact(full_ref[NB:, here], inv_ref[...], NT)
             row = lax.broadcasted_iota(jnp.int32, column.shape, 0)
-            below = jnp.where(row >= (p + 1) * NB, column, 0.0)
-            full_ref[:, here] = below
+            below = jnp.where(row >= p * NB, column, 0.0)
+            full_ref[NB:, here] = below
 
             @pl.when(p + 1 < nblk)
             def _():
                 for j in range(1, nblk):
                     @pl.when(p < j)
                     def _():
-                        full_ref[j * NB :, sl(j)] -= dot_exact(below[j * NB :, :], below[sl(j), :], NT)
+                        full_ref[j * NB :, sl(j)] -= dot_exact(below[(j - 1) * NB :, :], below[sl(j - 1), :], NT)
 
             full_ref[here, here] = up_ref[...].T
             return carry
@@ -258,12 +258,15 @@
                 full_ref[sl(i), sl(j)] = b
                 if j < i:
                     full_ref[sl(j), sl(i)] = b.T
-        basis_ref[...] = start_ref[...]
-
-        def step(_, carry):
-            image = dot_exact(full_ref[...], basis_ref[...])
-            cholesky_block(dot_exact(image, image, TN), inv_ref)
-            basis_ref[...] = dot_exact(image, inv_ref[...], NT)
+        basis_ref[...] = dot_exact(full_ref[...], start_ref[...])
+
+        def step(n, carry):
+            image = basis_ref[...]
+            projected = dot_exact(image, image, TN)
+            ahead = dot_exact(full_ref[...], image)
+            cholesky_block(projected, inv_ref)
+            last = n == ITERS - 1
+            basis_ref[...] = dot_exact(jnp.where(last, image, ahead), inv_ref[...], NT)
             return carry
 
         lax.fori_loop(0, ITERS, step, 0)

time: 148 us -> 147 us (level)
  no operation moved by 1% of the time
where the time goes in v5:
time: 147 us
  waiting for transfers between devices  48.3 us (33%)
  Pallas kernels  30.8 us (21%)
  starting transfers between devices  29.4 us (20%)
  blocking collectives  26.7 us (18%)
  local copies, waits for them, and re-layouts  9.61 us (7%)
    ppermute x15, waiting for transfers between devices, shift(): return lax.ppermute(value, axis, [(i, (i + by) % n) for i in range(n)])  41.3 us
    ppermute x15, starting transfers between devices, shift(): return lax.ppermute(value, axis, [(i, (i + by) % n) for i in range(n)])  26.8 us
    pallas_call x1, Pallas kernels, factorize(): pl.pallas_call(functools.partial(factor_kernel, scale), in_specs=[SMEM, V...  18.7 us
    all_to_all x1, blocking collectives, sum_everywhere(): lax.all_to_all(mine.reshape(n, rows // n, lanes), plane, 0, 0, tiled=True)  14.4 us
    all_to_all x1, blocking collectives, spread_out(): return lax.all_to_all(copies, axes, 0, 0, tiled=True)  12.3 us
    unnamed x14, local copies, waits for them, and re-layouts  7.92 us
    pallas_call x2, Pallas kernels, gram_lower(): pl.pallas_call(functools.partial(gram_kernel, prior is not None, final),...  5.39 us
    ppermute x4, waiting for transfers between devices, swap_cores(): return lax.ppermute(value, 'core', [(0, 1), (1, 0)])  5.19 us
  transfers between devices with their start and end apart: 20, of which 13 were waited for; matrix products, arithmetic and copies ran while one was open for 1% of the time, Pallas kernels for 6%

profile of v5, /device:TPU:6, one launch (start us, length us, event | category | flops | bytes accessed | tf_op | source)
XLA Modules:
  0.0 146.6 jit_solution(11018475639617165321)
XLA Ops:
  0.6 1.5 %constant_dynamic-slice_fusion = (f32[128,1024]{1,0:T(8,128)S(1)}, f32[128,1024]{1,0:T(8,128)S(1)}, f32[128,1024]{1,0:T(8,128)S(1)}) fusion(f32[128,8192]{1,0:T(8,128)} %source_ref.2, u32[]{:T(128)S(6)} %mul.27, u32[]{:T(128)S(6)} %mul.25, u32[]{:T(128)S(6)} %mul.26), kind=kLoop, calls=%fused_computation.10 | loop fusion | bytes 3145740 | tf_op jit(solution)/shard_map/dynamic_slice | solution.py:358
  2.1 1.5 %collective-permute-start.4 = (f32[128,1024]{1,0:T(8,128)S(1)}, f32[128,1024]{1,0:T(8,128)S(1)}, u32[]{:S(2)}, u32[]{:S(2)}) collective-permute-start(f32[128,1024]{1,0:T(8,128)S(1)} %get-tuple-element.50), channel_id=1, source_target_pairs={{0,128},{64,192},{128,0},{192,64},{1,129},{65,193},{129,1},{193,65... | collective-permute-start | bytes 1572872 | tf_op jit(solution)/shard_map/ppermute | solution.py:323
  3.6 2.1 %collective-permute-start.3 = (f32[128,1024]{1,0:T(8,128)S(1)}, f32[128,1024]{1,0:T(8,128)S(1)}, u32[]{:S(2)}, u32[]{:S(2)}) collective-permute-start(f32[128,1024]{1,0:T(8,128)S(1)} %get-tuple-element.51), channel_id=1, source_target_pairs={{0,64},{64,128},{128,192},{192,0},{1,65},{65,129},{129,193},{193,1... | collective-permute-start | bytes 1572872 | tf_op jit(solution)/shard_map/ppermute | solution.py:323
  5.8 2.2 %copy-done = f32[128,8192]{1,0:T(8,128)S(1)} copy-done((f32[128,8192]{1,0:T(8,128)S(1)}, f32[128,8192]{1,0:T(8,128)}, u32[]{:S(2)}) %copy-start) | copy-done | bytes 4194328
  8.0 0.7 column_slices.3
  8.7 2.1 %collective-permute-start.1 = (f32[128,1024]{1,0:T(8,128)S(1)}, f32[128,1024]{1,0:T(8,128)S(1)}, u32[]{:S(2)}, u32[]{:S(2)}) collective-permute-start(f32[128,1024]{1,0:T(8,128)S(1)} %get-tuple-element.27), channel_id=1, source_target_pairs={{0,128},{64,192},{128,0},{192,64},{1,129},{65,193},{129,1},{193,65... | collective-permute-start | bytes 1572872 | tf_op jit(solution)/shard_map/ppermute | solution.py:323
  10.8 2.2 %collective-permute-start = (f32[128,1024]{1,0:T(8,128)S(1)}, f32[128,1024]{1,0:T(8,128)S(1)}, u32[]{:S(2)}, u32[]{:S(2)}) collective-permute-start(f32[128,1024]{1,0:T(8,128)S(1)} %get-tuple-element.29), channel_id=1, source_target_pairs={{0,64},{64,128},{128,192},{192,0},{1,65},{65,129},{129,193},{193,1... | collective-permute-start | bytes 1572872 | tf_op jit(solution)/shard_map/ppermute | solution.py:323
  13.0 5.5 %collective-permute-done.4.refs_2_ = f32[128,1024]{1,0:T(8,128)S(1)} collective-permute-done((f32[128,1024]{1,0:T(8,128)S(1)}, f32[128,1024]{1,0:T(8,128)S(1)}, u32[]{:S(2)}, u32[]{:S(2)}) %collective-permute-start.4) | collective-permute-done | bytes 524320 | tf_op jit(solution)/shard_map/ppermute | solution.py:323
  18.6 0.8 collective-permute-start.2
  19.3 0.6 column_slices.5.refs_0_
  20.0 0.6 column_slices.4.refs_0_
  20.6 8.8 %collective-permute-done.3.refs_1_ = f32[128,1024]{1,0:T(8,128)S(1)} collective-permute-done((f32[128,1024]{1,0:T(8,128)S(1)}, f32[128,1024]{1,0:T(8,128)S(1)}, u32[]{:S(2)}, u32[]{:S(2)}) %collective-permute-start.3) | collective-permute-done | bytes 524320 | tf_op jit(solution)/shard_map/ppermute | solution.py:323
  29.4 0.5 collective-permute-done.5.refs_3_
  29.9 0.8 copy-done.3
  30.6 1.0 copy-done.4
  31.7 2.7 %gram_lower.2 = (bf16[512,2048]{1,0:T(8,128)(2,1)S(1)}, f32[1280,128]{1,0:T(8,128)S(1)}) custom-call(s32[2]{0:T(128)S(1)} %pad_add_fusion.place_ref, f32[128,1024]{1,0:T(8,128)S(1)} %column_slices.5.refs_0_, f32[128,1024]{1,0:T(8,128)S(1)} %collective-permute-done.3.refs_1_, f32[128,1024]{1,0:T(8,128)S(1)} %collective-permute-done.4.refs_2_, ...), custom_call_target="tpu_custom_call" | custom-call | tf_op jit(solution)/shard_map/gram_lower/pallas_call | solution.py:169
  34.4 6.7 %collective-permute-done.1.refs_2_ = f32[128,1024]{1,0:T(8,128)S(1)} collective-permute-done((f32[128,1024]{1,0:T(8,128)S(1)}, f32[128,1024]{1,0:T(8,128)S(1)}, u32[]{:S(2)}, u32[]{:S(2)}) %collective-permute-start.1) | collective-permute-done | bytes 524320 | tf_op jit(solution)/shard_map/ppermute | solution.py:323
  41.1 7.7 %collective-permute-done.refs_1_ = f32[128,1024]{1,0:T(8,128)S(1)} collective-permute-done((f32[128,1024]{1,0:T(8,128)S(1)}, f32[128,1024]{1,0:T(8,128)S(1)}, u32[]{:S(2)}, u32[]{:S(2)}) %collective-permute-start) | collective-permute-done | bytes 524320 | tf_op jit(solution)/shard_map/ppermute | solution.py:323
  48.7 2.3 %collective-permute-done.2.refs_3_ = f32[128,1024]{1,0:T(8,128)S(1)} collective-permute-done((f32[128,1024]{1,0:T(8,128)S(1)}, f32[128,1024]{1,0:T(8,128)S(1)}, u32[]{:S(2)}, u32[]{:S(2)}) %collective-permute-start.2) | collective-permute-done | bytes 524320 | tf_op jit(solution)/shard_map/ppermute | solution.py:323
  51.1 2.7 %gram_lower.3 = (bf16[512,2048]{1,0:T(8,128)(2,1)S(1)}, f32[640,128]{1,0:T(8,128)S(1)}, f32[640,128]{1,0:T(8,128)S(1)}) custom-call(s32[2]{0:T(128)S(1)} %pad_add_fusion.place_ref, f32[128,1024]{1,0:T(8,128)S(1)} %column_slices.4.refs_0_, f32[128,1024]{1,0:T(8,128)S(1)} %collective-permute-done.refs_1_, f32[128,1024]{1,0:T(8,128)S(1)} %collective-permute-done.1.refs_2_, ...), custom_call_target="tpu_custom_call" | custom-call | tf_op jit(solution)/shard_map/gram_lower/pallas_call | solution.py:169
  53.8 1.3 copy-done.1
  55.2 1.6 %collective-permute-done.6 = f32[640,128]{1,0:T(8,128)S(1)} collective-permute-done((f32[640,128]{1,0:T(8,128)S(1)}, f32[640,128]{1,0:T(8,128)S(1)}, u32[]{:S(2)}, u32[]{:S(2)}) %collective-permute-start.6) | collective-permute-done | bytes 327712 | tf_op jit(solution)/shard_map/ppermute | solution.py:318
  56.8 14.4 %all_to_all.10 = f32[16,40,128]{2,1,0:T(8,128)S(1)} all-to-all(f32[16,40,128]{2,1,0:T(8,128)S(1)} %bitcast.6), channel_id=1, replica_groups=mesh['mode'=4,'y'=4,'z'=8,'core'=2] {'mode','y'}, dimensions={0} | all-to-all | bytes 655360 | tf_op jit(solution)/shard_map/all_to_all | solution.py:343
  71.3 2.0 %collective-permute-start.7 = (f32[40,128]{1,0:T(8,128)S(1)}, f32[40,128]{1,0:T(8,128)S(1)}, u32[]{:S(2)}, u32[]{:S(2)}) collective-permute-start(f32[40,128]{1,0:T(8,128)S(1)} %reduce_sum.9), channel_id=1, source_target_pairs={{0,2},{2,0},{4,6},{6,4},{8,10},{10,8},{12,14},{14,12},{1,3},{3,1},... | collective-permute-start | bytes 61448 | tf_op jit(solution)/shard_map/ppermute | solution.py:333
  73.3 1.9 %collective-permute-done.7 = f32[40,128]{1,0:T(8,128)S(1)} collective-permute-done((f32[40,128]{1,0:T(8,128)S(1)}, f32[40,128]{1,0:T(8,128)S(1)}, u32[]{:S(2)}, u32[]{:S(2)}) %collective-permute-start.7) | collective-permute-done | bytes 20512 | tf_op jit(solution)/shard_map/ppermute | solution.py:333
  75.1 6.3 %collective-permute-start.10 = (f32[40,128]{1,0:T(8,128)S(1)}, f32[40,128]{1,0:T(8,128)S(1)}, u32[]{:S(2)}, u32[]{:S(2)}) collective-permute-start(f32[40,128]{1,0:T(8,128)S(1)} %add.75), channel_id=1, source_target_pairs={{0,12},{2,14},{4,0},{6,2},{8,4},{10,6},{12,8},{14,10},{1,13},{3,15... | collective-permute-start | bytes 61448 | tf_op jit(solution)/shard_map/ppermute | solution.py:323
  81.4 1.1 collective-permute-start.8
  82.5 2.8 %collective-permute-start.9 = (f32[40,128]{1,0:T(8,128)S(1)}, f32[40,128]{1,0:T(8,128)S(1)}, u32[]{:S(2)}, u32[]{:S(2)}) collective-permute-start(f32[40,128]{1,0:T(8,128)S(1)} %add.75), channel_id=1, source_target_pairs={{0,4},{2,6},{4,8},{6,10},{8,12},{10,14},{12,0},{14,2},{1,5},{3,7},... | collective-permute-start | bytes 61448 | tf_op jit(solution)/shard_map/ppermute | solution.py:323
  85.3 3.8 %collective-permute-done.8 = f32[40,128]{1,0:T(8,128)S(1)} collective-permute-done((f32[40,128]{1,0:T(8,128)S(1)}, f32[40,128]{1,0:T(8,128)S(1)}, u32[]{:S(2)}, u32[]{:S(2)}) %collective-permute-start.8) | collective-permute-done | bytes 20512 | tf_op jit(solution)/shard_map/ppermute | solution.py:323
  89.2 12.3 %all_to_all.11 = f32[16,40,128]{2,1,0:T(8,128)S(1)} all-to-all(f32[16,40,128]{2,1,0:T(8,128)S(1)} %broadcast_in_dim.10), channel_id=1, replica_groups=mesh['mode'=4,'y'=4,'z'=8,'core'=2] {'mode','y'}, dimensions={0} | all-to-all | bytes 655360 | tf_op jit(solution)/shard_map/all_to_all | solution.py:329
  101.5 1.6 %collective-permute-done.11.other_ref = f32[640,128]{1,0:T(8,128)S(1)} collective-permute-done((f32[640,128]{1,0:T(8,128)S(1)}, f32[640,128]{1,0:T(8,128)S(1)}, u32[]{:S(2)}, u32[]{:S(2)}) %collective-permute-start.11) | collective-permute-done | bytes 327712 | tf_op jit(solution)/shard_map/ppermute | solution.py:318
  103.1 18.7 %factorize.1 = (f32[1280,128]{1,0:T(8,128)S(1)}, f32[512,128]{1,0:T(8,128)S(1)}) custom-call(s32[2]{0:T(128)S(1)} %pad_add_fusion.place_ref, f32[640,128]{1,0:T(8,128)S(1)} %bitcast.5, f32[640,128]{1,0:T(8,128)S(1)} %collective-permute-done.11.other_ref, f32[512,128]{1,0:T(8,128)S(1)} %copy-done.5), custom_call_target="tpu_custom_call" | custom-call | tf_op jit(solution)/shard_map/factorize/pallas_call | solution.py:278
  121.8 0.1 collective-permute-start.12
  121.9 0.5 collective-permute-start.13
  122.4 2.0 %collective-permute-done.13.other_ref = f32[512,128]{1,0:T(8,128)S(1)} collective-permute-done((f32[512,128]{1,0:T(8,128)S(1)}, f32[512,128]{1,0:T(8,128)S(1)}, u32[]{:S(2)}, u32[]{:S(2)}) %collective-permute-start.13) | collective-permute-done | bytes 262176 | tf_op jit(solution)/shard_map/ppermute | solution.py:318
  124.4 1.3 core_rows.3
  125.7 1.8 %collective-permute-start.14 = (f32[32,1024]{1,0:T(8,128)S(1)}, f32[32,1024]{1,0:T(8,128)S(1)}, u32[]{:S(2)}, u32[]{:S(2)}) collective-permute-start(f32[32,1024]{1,0:T(8,128)S(1)} %get-tuple-element.42), channel_id=1, source_target_pairs={{0,128},{64,192},{128,0},{192,64},{1,129},{65,193},{129,1},{193,65... | collective-permute-start | bytes 393224 | tf_op jit(solution)/shard_map/ppermute | solution.py:323
  127.5 1.7 %collective-permute-start.15 = (f32[32,1024]{1,0:T(8,128)S(1)}, f32[32,1024]{1,0:T(8,128)S(1)}, u32[]{:S(2)}, u32[]{:S(2)}) collective-permute-start(f32[32,1024]{1,0:T(8,128)S(1)} %get-tuple-element.43), channel_id=1, source_target_pairs={{0,64},{64,128},{128,192},{192,0},{1,65},{65,129},{129,193},{193,1... | collective-permute-start | bytes 393224 | tf_op jit(solution)/shard_map/ppermute | solution.py:323
  129.2 0.3 collective-permute-start.16
  129.5 1.6 %copy-done.2 = bf16[512,2048]{1,0:T(8,128)(2,1)S(1)} copy-done((bf16[512,2048]{1,0:T(8,128)(2,1)S(1)}, bf16[512,2048]{1,0:T(8,128)(2,1)}, u32[]{:S(2)}) %copy-start.2) | copy-done | bytes 2097176
  131.1 1.3 core_rows.2
  132.4 1.9 %collective-permute-start.17 = (f32[32,1024]{1,0:T(8,128)S(1)}, f32[32,1024]{1,0:T(8,128)S(1)}, u32[]{:S(2)}, u32[]{:S(2)}) collective-permute-start(f32[32,1024]{1,0:T(8,128)S(1)} %get-tuple-element.46), channel_id=1, source_target_pairs={{0,128},{64,192},{128,0},{192,64},{1,129},{65,193},{129,1},{193,65... | collective-permute-start | bytes 393224 | tf_op jit(solution)/shard_map/ppermute | solution.py:323
  134.4 0.7 broadcast_select_fusion
  135.1 2.1 %collective-permute-start.18 = (f32[32,1024]{1,0:T(8,128)S(1)}, f32[32,1024]{1,0:T(8,128)S(1)}, u32[]{:S(2)}, u32[]{:S(2)}) collective-permute-start(f32[32,1024]{1,0:T(8,128)S(1)} %get-tuple-element.47), channel_id=1, source_target_pairs={{0,64},{64,128},{128,192},{192,0},{1,65},{65,129},{129,193},{193,1... | collective-permute-start | bytes 393224 | tf_op jit(solution)/shard_map/ppermute | solution.py:323
  137.2 2.2 %unpack_triangle.1 = f32[512,512]{1,0:T(8,128)} custom-call(s32[2]{0:T(128)S(1)} %pad_add_fusion.place_ref, f32[1280,128]{1,0:T(8,128)S(1)} %get-tuple-element.34.mine_ref, f32[1280,128]{1,0:T(8,128)} %collective-permute-done.12.other_ref), custom_call_target="tpu_custom_call" | custom-call | tf_op jit(solution)/shard_map/unpack_triangle/pallas_call | solution.py:306
  139.6 2.2 %collective-permute-done.18 = f32[32,1024]{1,0:T(8,128)S(1)} collective-permute-done((f32[32,1024]{1,0:T(8,128)S(1)}, f32[32,1024]{1,0:T(8,128)S(1)}, u32[]{:S(2)}, u32[]{:S(2)}) %collective-permute-start.18) | collective-permute-done | bytes 131104 | tf_op jit(solution)/shard_map/ppermute | solution.py:323
  141.8 3.8 %collective-permute-done.19 = f32[32,1024]{1,0:T(8,128)S(1)} collective-permute-done((f32[32,1024]{1,0:T(8,128)S(1)}, f32[32,1024]{1,0:T(8,128)S(1)}, u32[]{:S(2)}, u32[]{:S(2)}) %collective-permute-start.19) | collective-permute-done | bytes 131104 | tf_op jit(solution)/shard_map/ppermute | solution.py:323
  145.6 1.0 copy-done.6
  (34 shorter events, 0.4 us)
Async XLA Ops:
  2.1 16.4 %collective-permute-start.4 = (f32[128,1024]{1,0:T(8,128)S(1)}, f32[128,1024]{1,0:T(8,128)S(1)}, u32[]{:S(2)}, u32[]{:S(2)}) collective-permute-start(f32[128,1024]{1,0:T(8,128)S(1)} %get-tuple-element.50), channel_id=1, source_target_pairs={{0,128},{64,192},{128,0},{192,64},{1,129},{65,193},{129,1},{193,65... | collective-permute-start | bytes 1572872 | tf_op jit(solution)/shard_map/ppermute | solution.py:323
  3.6 25.8 %collective-permute-start.3 = (f32[128,1024]{1,0:T(8,128)S(1)}, f32[128,1024]{1,0:T(8,128)S(1)}, u32[]{:S(2)}, u32[]{:S(2)}) collective-permute-start(f32[128,1024]{1,0:T(8,128)S(1)} %get-tuple-element.51), channel_id=1, source_target_pairs={{0,64},{64,128},{128,192},{192,0},{1,65},{65,129},{129,193},{193,1... | collective-permute-start | bytes 1572872 | tf_op jit(solution)/shard_map/ppermute | solution.py:323
  5.7 24.2 %collective-permute-start.5 = (f32[128,1024]{1,0:T(8,128)S(1)}, f32[128,1024]{1,0:T(8,128)S(1)}, u32[]{:S(2)}, u32[]{:S(2)}) collective-permute-start(f32[128,1024]{1,0:T(8,128)S(1)} %get-tuple-element.49), channel_id=1, source_target_pairs={{0,192},{64,0},{128,64},{192,128},{1,193},{65,1},{129,65},{193,129... | collective-permute-start | bytes 1572872 | tf_op jit(solution)/shard_map/ppermute | solution.py:323
  5.8 2.2 %copy-start = (f32[128,8192]{1,0:T(8,128)S(1)}, f32[128,8192]{1,0:T(8,128)}, u32[]{:S(2)}) copy-start(f32[128,8192]{1,0:T(8,128)} %source_ref.2) | copy-start | bytes 12582916
  8.7 32.4 %collective-permute-start.1 = (f32[128,1024]{1,0:T(8,128)S(1)}, f32[128,1024]{1,0:T(8,128)S(1)}, u32[]{:S(2)}, u32[]{:S(2)}) collective-permute-start(f32[128,1024]{1,0:T(8,128)S(1)} %get-tuple-element.27), channel_id=1, source_target_pairs={{0,128},{64,192},{128,0},{192,64},{1,129},{65,193},{129,1},{193,65... | collective-permute-start | bytes 1572872 | tf_op jit(solution)/shard_map/ppermute | solution.py:323
  10.8 37.9 %collective-permute-start = (f32[128,1024]{1,0:T(8,128)S(1)}, f32[128,1024]{1,0:T(8,128)S(1)}, u32[]{:S(2)}, u32[]{:S(2)}) collective-permute-start(f32[128,1024]{1,0:T(8,128)S(1)} %get-tuple-element.29), channel_id=1, source_target_pairs={{0,64},{64,128},{128,192},{192,0},{1,65},{65,129},{129,193},{193,1... | collective-permute-start | bytes 1572872 | tf_op jit(solution)/shard_map/ppermute | solution.py:323
  18.6 32.5 %collective-permute-start.2 = (f32[128,1024]{1,0:T(8,128)S(1)}, f32[128,1024]{1,0:T(8,128)S(1)}, u32[]{:S(2)}, u32[]{:S(2)}) collective-permute-start(f32[128,1024]{1,0:T(8,128)S(1)} %get-tuple-element.30), channel_id=1, source_target_pairs={{0,192},{64,0},{128,64},{192,128},{1,193},{65,1},{129,65},{193,129... | collective-permute-start | bytes 1572872 | tf_op jit(solution)/shard_map/ppermute | solution.py:323
  19.9 83.2 %copy-start.5 = (f32[512,128]{1,0:T(8,128)S(1)}, f32[512,128]{1,0:T(8,128)}, u32[]{:S(2)}) copy-start(f32[512,128]{1,0:T(8,128)} %start_ref.1) | copy-start | bytes 786436
  29.9 0.8 copy-start.3
  30.6 1.0 copy-start.4
  53.8 1.3 copy-start.1
  55.2 1.6 %collective-permute-start.6 = (f32[640,128]{1,0:T(8,128)S(1)}, f32[640,128]{1,0:T(8,128)S(1)}, u32[]{:S(2)}, u32[]{:S(2)}) collective-permute-start(f32[640,128]{1,0:T(8,128)S(1)} %get-tuple-element.33), channel_id=1, source_target_pairs={{0,1},{1,0},{2,3},{3,2},{4,5},{5,4},{6,7},{7,6},{8,9},{9,8},{10,11... | collective-permute-start | bytes 983048 | tf_op jit(solution)/shard_map/ppermute | solution.py:318
  71.3 3.9 %collective-permute-start.7 = (f32[40,128]{1,0:T(8,128)S(1)}, f32[40,128]{1,0:T(8,128)S(1)}, u32[]{:S(2)}, u32[]{:S(2)}) collective-permute-start(f32[40,128]{1,0:T(8,128)S(1)} %reduce_sum.9), channel_id=1, source_target_pairs={{0,2},{2,0},{4,6},{6,4},{8,10},{10,8},{12,14},{14,12},{1,3},{3,1},... | collective-permute-start | bytes 61448 | tf_op jit(solution)/shard_map/ppermute | solution.py:333
  75.1 10.2 %collective-permute-start.10 = (f32[40,128]{1,0:T(8,128)S(1)}, f32[40,128]{1,0:T(8,128)S(1)}, u32[]{:S(2)}, u32[]{:S(2)}) collective-permute-start(f32[40,128]{1,0:T(8,128)S(1)} %add.75), channel_id=1, source_target_pairs={{0,12},{2,14},{4,0},{6,2},{8,4},{10,6},{12,8},{14,10},{1,13},{3,15... | collective-permute-start | bytes 61448 | tf_op jit(solution)/shard_map/ppermute | solution.py:323
  81.4 7.7 %collective-permute-start.8 = (f32[40,128]{1,0:T(8,128)S(1)}, f32[40,128]{1,0:T(8,128)S(1)}, u32[]{:S(2)}, u32[]{:S(2)}) collective-permute-start(f32[40,128]{1,0:T(8,128)S(1)} %add.75), channel_id=1, source_target_pairs={{0,8},{2,10},{4,12},{6,14},{8,0},{10,2},{12,4},{14,6},{1,9},{3,11}... | collective-permute-start | bytes 61448 | tf_op jit(solution)/shard_map/ppermute | solution.py:323
  82.5 6.6 %collective-permute-start.9 = (f32[40,128]{1,0:T(8,128)S(1)}, f32[40,128]{1,0:T(8,128)S(1)}, u32[]{:S(2)}, u32[]{:S(2)}) collective-permute-start(f32[40,128]{1,0:T(8,128)S(1)} %add.75), channel_id=1, source_target_pairs={{0,4},{2,6},{4,8},{6,10},{8,12},{10,14},{12,0},{14,2},{1,5},{3,7},... | collective-permute-start | bytes 61448 | tf_op jit(solution)/shard_map/ppermute | solution.py:323
  101.5 1.6 %collective-permute-start.11 = (f32[640,128]{1,0:T(8,128)S(1)}, f32[640,128]{1,0:T(8,128)S(1)}, u32[]{:S(2)}, u32[]{:S(2)}) collective-permute-start(f32[640,128]{1,0:T(8,128)S(1)} %bitcast.4), channel_id=1, source_target_pairs={{0,1},{1,0},{2,3},{3,2},{4,5},{5,4},{6,7},{7,6},{8,9},{9,8},{10,11... | collective-permute-start | bytes 983048 | tf_op jit(solution)/shard_map/ppermute | solution.py:318
  121.8 13.3 %collective-permute-start.12 = (f32[1280,128]{1,0:T(8,128)S(1)}, f32[1280,128]{1,0:T(8,128)}, u32[]{:S(2)}, u32[]{:S(2)}) collective-permute-start(f32[1280,128]{1,0:T(8,128)S(1)} %get-tuple-element.34.mine_ref), channel_id=1, source_target_pairs={{0,1},{1,0},{2,3},{3,2},{4,5},{5,4},{6,7},{7,6},{8,9},{9,8},{10,11... | collective-permute-start | bytes 1966088 | tf_op jit(solution)/shard_map/ppermute | solution.py:318
  121.9 2.5 %collective-permute-start.13 = (f32[512,128]{1,0:T(8,128)S(1)}, f32[512,128]{1,0:T(8,128)S(1)}, u32[]{:S(2)}, u32[]{:S(2)}) collective-permute-start(f32[512,128]{1,0:T(8,128)S(1)} %get-tuple-element.35.mine_ref), channel_id=1, source_target_pairs={{0,1},{1,0},{2,3},{3,2},{4,5},{5,4},{6,7},{7,6},{8,9},{9,8},{10,11... | collective-permute-start | bytes 786440 | tf_op jit(solution)/shard_map/ppermute | solution.py:318
  125.7 13.7 %collective-permute-start.14 = (f32[32,1024]{1,0:T(8,128)S(1)}, f32[32,1024]{1,0:T(8,128)S(1)}, u32[]{:S(2)}, u32[]{:S(2)}) collective-permute-start(f32[32,1024]{1,0:T(8,128)S(1)} %get-tuple-element.42), channel_id=1, source_target_pairs={{0,128},{64,192},{128,0},{192,64},{1,129},{65,193},{129,1},{193,65... | collective-permute-start | bytes 393224 | tf_op jit(solution)/shard_map/ppermute | solution.py:323
  127.5 12.0 %collective-permute-start.15 = (f32[32,1024]{1,0:T(8,128)S(1)}, f32[32,1024]{1,0:T(8,128)S(1)}, u32[]{:S(2)}, u32[]{:S(2)}) collective-permute-start(f32[32,1024]{1,0:T(8,128)S(1)} %get-tuple-element.43), channel_id=1, source_target_pairs={{0,64},{64,128},{128,192},{192,0},{1,65},{65,129},{129,193},{193,1... | collective-permute-start | bytes 393224 | tf_op jit(solution)/shard_map/ppermute | solution.py:323
  129.2 10.3 %collective-permute-start.16 = (f32[32,1024]{1,0:T(8,128)S(1)}, f32[32,1024]{1,0:T(8,128)S(1)}, u32[]{:S(2)}, u32[]{:S(2)}) collective-permute-start(f32[32,1024]{1,0:T(8,128)S(1)} %get-tuple-element.44), channel_id=1, source_target_pairs={{0,192},{64,0},{128,64},{192,128},{1,193},{65,1},{129,65},{193,129... | collective-permute-start | bytes 393224 | tf_op jit(solution)/shard_map/ppermute | solution.py:323
  129.5 1.6 %copy-start.2 = (bf16[512,2048]{1,0:T(8,128)(2,1)S(1)}, bf16[512,2048]{1,0:T(8,128)(2,1)}, u32[]{:S(2)}) copy-start(bf16[512,2048]{1,0:T(8,128)(2,1)} %copy-done.1) | copy-start | bytes 6291460
  132.4 7.2 %collective-permute-start.17 = (f32[32,1024]{1,0:T(8,128)S(1)}, f32[32,1024]{1,0:T(8,128)S(1)}, u32[]{:S(2)}, u32[]{:S(2)}) collective-permute-start(f32[32,1024]{1,0:T(8,128)S(1)} %get-tuple-element.46), channel_id=1, source_target_pairs={{0,128},{64,192},{128,0},{192,64},{1,129},{65,193},{129,1},{193,65... | collective-permute-start | bytes 393224 | tf_op jit(solution)/shard_map/ppermute | solution.py:323
  135.1 6.7 %collective-permute-start.18 = (f32[32,1024]{1,0:T(8,128)S(1)}, f32[32,1024]{1,0:T(8,128)S(1)}, u32[]{:S(2)}, u32[]{:S(2)}) collective-permute-start(f32[32,1024]{1,0:T(8,128)S(1)} %get-tuple-element.47), channel_id=1, source_target_pairs={{0,64},{64,128},{128,192},{192,0},{1,65},{65,129},{129,193},{193,1... | collective-permute-start | bytes 393224 | tf_op jit(solution)/shard_map/ppermute | solution.py:323
  139.4 6.2 %collective-permute-start.19 = (f32[32,1024]{1,0:T(8,128)S(1)}, f32[32,1024]{1,0:T(8,128)S(1)}, u32[]{:S(2)}, u32[]{:S(2)}) collective-permute-start(f32[32,1024]{1,0:T(8,128)S(1)} %get-tuple-element.48), channel_id=1, source_target_pairs={{0,192},{64,0},{128,64},{192,128},{1,193},{65,1},{129,65},{193,129... | collective-permute-start | bytes 393224 | tf_op jit(solution)/shard_map/ppermute | solution.py:323
  145.6 1.0 copy-start.6
